TPU v7x, 32 devices: a whole 2x2x4 slice. The times are simulated.
32 devices in a mesh: lat: 4 (over y, x), lon: 8 (over z, core).
Axes of the slice: x: 2, y: 2, z: 4, core: 2. Of those that a mesh axis runs over, the one named last changes fastest.
Arguments:
- grad_rows: bfloat16 [32768, 128], P(('lat', 'lon')), may hold values from -6 to 6
- owner: int32 [32768, 1], P(('lat', 'lon')), may hold values from 0 to 31; in each aligned block of 1024 rows (0 to 1023, 1024 to 2047, ...) at most 64 rows name the same one
- lat_offset: int32 [32768], P(('lat', 'lon')), may hold values from 0 to 63
- lon_offset: int32 [32768], P(('lat', 'lon')), may hold values from 0 to 127
- position: bfloat16 [32768, 2], P(('lat', 'lon')), may hold values from 0 to 1
- live_count: int32 [32], P(('lat', 'lon')), may hold values from 512 to 1024
- features: bfloat16 [256, 1024, 128], P('lat', 'lon'), may hold values from -6 to 6
- conv_weight: bfloat16 [3, 3, 128, 128], replicated, may hold values from -0.1875 to 0.1875
Outputs:
- input_grad: bfloat16 [256, 1024, 128], P('lat', 'lon')
- weight_grad: float32 [3, 3, 128, 128], replicated
Inputs may be any that keep to these rules, and one draw needn't show every extreme that they name: `owner`: among the 1024 rows of one device no tile is named more than 64 times, a bound that some block reaches. `live_count`: entry k counts the real rows among the rows of device k, which come first.
All inputs are finite; a program needn't handle non-finite values.
Results may differ from a plain program's by a relative error of at most 0.012.
Values may be sent and summed in bfloat16 or wider, within the bound.
A program may use at most 128 MiB of HBM per device.

v0:
```python
import functools
import math

import jax
import jax.numpy as jnp
from jax import lax
from jax.experimental import pallas as pl
from jax.experimental.pallas import tpu as pltpu
from jax.sharding import PartitionSpec as P

rbf_scale = 1.5
taps = 8
before = 3
after = taps - 1 - before
geom_rows = 8
f32 = jnp.float32
bf16 = jnp.bfloat16


def pack_kernel(
    capacity,
    lat_total,
    lon_total,
    live_ref,
    rows_ref,
    owner_ref,
    lat_ref,
    lon_ref,
    pos_ref,
    out_ref,
    held,
    tally,
    send_sem,
    recv_sem,
):
    devices = out_ref.shape[0]
    row_total, channels = rows_ref.shape
    me = lax.axis_index("lat") * lon_total + lax.axis_index("lon")

    def place(peer):
        return (peer // lon_total, peer % lon_total)

    barrier = pltpu.get_barrier_semaphore()

    def greet(k, _):
        pl.semaphore_signal(
            barrier, inc=1, device_id=place((me + k) % devices), device_id_type=pl.DeviceIdType.MESH
        )
        return 0

    lax.fori_loop(1, devices, greet, 0)
    live = lax.broadcasted_iota(jnp.int32, (1, row_total), 1) < live_ref[0]
    owner = jnp.where(live, owner_ref[...], devices)
    match = lax.broadcasted_iota(jnp.int32, (devices, row_total), 0) == owner
    match = jnp.where(match, 1.0, 0.0)
    tally[...] = jnp.broadcast_to(jnp.sum(match, axis=1, keepdims=True), tally.shape)
    upper = lax.broadcasted_iota(jnp.int32, (row_total, row_total), 0) < lax.broadcasted_iota(
        jnp.int32, (row_total, row_total), 1
    )
    upper = jnp.where(upper, 1.0, 0.0).astype(bf16)
    earlier = jnp.dot(match.astype(bf16), upper, preferred_element_type=f32)
    rank = jnp.sum(earlier * match, axis=0, keepdims=True).astype(jnp.int32)
    slot = owner * capacity + rank
    geometry = jnp.concatenate(
        [
            pos_ref[...].astype(f32),
            lat_ref[...].astype(f32),
            lon_ref[...].astype(f32),
            jnp.zeros((geom_rows - 4, row_total), f32),
        ],
        axis=0,
    ).astype(bf16)
    group = math.gcd(devices, max(1, 256 // capacity))
    groups = devices // group
    line = lax.broadcasted_iota(jnp.int32, (group * capacity, row_total), 0)
    row_line = lax.broadcasted_iota(jnp.int32, (geom_rows, capacity), 0)

    def build(first):
        hit = jnp.where(line == slot - first * capacity, 1.0, 0.0).astype(bf16)
        placed = jnp.dot(hit, rows_ref[...], preferred_element_type=f32).astype(bf16)
        info = lax.dot_general(
            geometry, hit, (((1,), (1,)), ((), ())), preferred_element_type=f32
        )
        for i in range(group):
            held[first + i, 0:capacity, :] = placed[i * capacity : (i + 1) * capacity]
            held[first + i, capacity : capacity + geom_rows, 0:capacity] = jnp.where(
                row_line == 4,
                tally[pl.ds(first + i, 1), 0:capacity],
                info[:, i * capacity : (i + 1) * capacity],
            ).astype(bf16)

    def copy_to(peer, slot_at):
        return pltpu.make_async_remote_copy(
            src_ref=held.at[peer],
            dst_ref=out_ref.at[slot_at],
            send_sem=send_sem.at[peer],
            recv_sem=recv_sem.at[slot_at],
            device_id=place(peer),
            device_id_type=pl.DeviceIdType.MESH,
        )

    def send(first):
        for i in range(group):
            peer = first + i

            @pl.when(peer != me)
            def _():
                copy_to(peer, me).start()

    odd = groups // 2

    def first_of(k):
        ahead = jnp.where(k < odd, 2 * k + 1, 2 * (k - odd))
        return ((me // group + ahead) % groups) * group

    build(first_of(0))
    pl.semaphore_wait(barrier, devices - 1)

    def work(k, _):
        build(first_of(k))
        send(first_of(k - 1))
        return 0

    lax.fori_loop(1, groups, work, 0)
    send(first_of(groups - 1))
    out_ref[me] = held[me]

    def each(fn):
        def body(k, _):
            fn((me + k) % devices)
            return 0

        lax.fori_loop(1, devices, body, 0)

    each(lambda peer: copy_to(peer, peer).wait_recv())
    each(lambda peer: copy_to(peer, me).wait_send())


def scatter_kernel(
    capacity,
    lanes,
    info_ref,
    msg_ref,
    own_ref,
    up_ref,
    down_ref,
    left_ref,
    right_ref,
    ul_ref,
    ur_ref,
    dl_ref,
    dr_ref,
    canvas,
    block,
):
    sources = msg_ref.shape[0]
    slots = sources * capacity
    rows, cols = own_ref.shape[0], own_ref.shape[1]
    tall = canvas.shape[1]
    inv = 1.0 / (2.0 * rbf_scale * rbf_scale)

    def clear(i, _):
        for j in range(lanes):
            canvas[j, i] = jnp.zeros(canvas.shape[2:], f32)
        return 0

    lax.fori_loop(0, tall, clear, 0)
    line = lax.broadcasted_iota(jnp.int32, (taps, canvas.shape[3]), 0).astype(f32) - before
    level = [math.exp(-((a - before) ** 2 - before**2) * inv) for a in range(taps)]

    def source(src, _):
        block[...] = msg_ref[src, 0:capacity, :].astype(f32)

        def prepare(i):
            terms = []
            for j in range(lanes):
                s = i * lanes + j
                at = src * capacity + s
                fa, fb = info_ref[at], info_ref[at + slots]
                d = line - fb
                t = jnp.exp(-(d * d + (before + fa) * (before + fa)) * inv) * block[pl.ds(s, 1), :]
                g = jnp.exp(jnp.full(t.shape, 2.0 * inv, f32) * fa)
                r = info_ref[at + 2 * slots].astype(jnp.int32)
                c = info_ref[at + 3 * slots].astype(jnp.int32)
                terms.append((r, c, t, g))
            return tuple(terms)

        trips = (info_ref[4 * slots + src * capacity].astype(jnp.int32) + lanes - 1) // lanes

        def step(i, terms):
            ahead = prepare(jnp.minimum(i + 1, trips - 1))
            sums = []
            for j, (r, c, t, g) in enumerate(terms):
                for a in range(taps):
                    sums.append(canvas[j, r + a, pl.ds(c, taps), :] + t * level[a])
                    t = t * g
            for j, (r, c, _, _) in enumerate(terms):
                for a in range(taps):
                    canvas[j, r + a, pl.ds(c, taps), :] = sums[j * taps + a]
            return ahead

        lax.fori_loop(0, trips, step, prepare(0))
        return 0

    lax.fori_loop(0, sources, source, 0)
    up, down = before + 1, after + 1
    inset = before - 1

    def total(i):
        whole = canvas[0, i]
        for j in range(1, lanes):
            whole = whole + canvas[j, i]
        canvas[0, i] = whole

    def finish(i, _):
        total(i)
        return 0

    lax.fori_loop(0, tall, finish, 0)

    def emit(i, _):
        own_ref[i] = canvas[0, i + inset, inset : inset + cols, :].astype(bf16)
        left_ref[i] = canvas[0, i + inset, 0:up, :].astype(bf16)
        right_ref[i] = canvas[0, i + inset, inset + cols - 2 : inset + cols - 2 + down, :].astype(bf16)
        return 0

    lax.fori_loop(0, rows, emit, 0)
    spans = ((0, up), (inset, cols), (inset + cols - 2, down))
    for count, first, refs in (
        (up, 0, (ul_ref, up_ref, ur_ref)),
        (down, inset + rows - 2, (dl_ref, down_ref, dr_ref)),
    ):
        for i in range(count):
            for (start, width), ref in zip(spans, refs):
                ref[i] = canvas[0, first + i, start : start + width, :].astype(bf16)


def conv_kernel(
    lat_total,
    lon_total,
    own_ref,
    *refs,
):
    strips, (feat_ref, weight_ref, ig_ref, wg_ref) = refs[:8], refs[8:12]
    landed = refs[12:20]
    (grid, windows, turned, total, flat, mixer, pieces, twin, parts, mine, gathered) = refs[20:31]
    halo_send, halo_recv, pair_send, pair_recv, part_send, part_recv, all_send, all_recv = refs[31:]
    rows, cols = own_ref.shape[0], own_ref.shape[1]
    tile_lat, tile_lon, channels = feat_ref.shape
    up, down = before + 1, after + 1
    devices = lat_total * lon_total
    lat, lon = lax.axis_index("lat"), lax.axis_index("lon")
    me = lat * lon_total + lon
    chips = devices // 2
    core, chip = me % 2, me // 2
    other = 1 - core

    def place(peer):
        return (peer // lon_total, peer % lon_total)

    barrier = pltpu.get_barrier_semaphore()

    def greet(k, _):
        pl.semaphore_signal(
            barrier, inc=1, device_id=place((me + k) % devices), device_id_type=pl.DeviceIdType.MESH
        )
        return 0

    lax.fori_loop(1, devices, greet, 0)

    def fill(i, _):
        grid[i, 0:cols, :] = own_ref[i].astype(f32)
        return 0

    lax.fori_loop(0, rows, fill, 0)
    pl.semaphore_wait(barrier, devices - 1)

    ways = ((-1, 0), (1, 0), (0, -1), (0, 1), (-1, -1), (-1, 1), (1, -1), (1, 1))
    halos = []
    for w, (da, db) in enumerate(ways):
        copy = pltpu.make_async_remote_copy(
            src_ref=strips[w],
            dst_ref=landed[w],
            send_sem=halo_send.at[w],
            recv_sem=halo_recv.at[w],
            device_id=((lat + da + lat_total) % lat_total, (lon + db + lon_total) % lon_total),
            device_id_type=pl.DeviceIdType.MESH,
        )
        sends = (lat + da >= 0) & (lat + da < lat_total)
        takes = (lat - da >= 0) & (lat - da < lat_total)
        halos.append((copy, sends, takes))

    def when(da, cond, fn):
        if da == 0:
            fn()
        else:
            pl.when(cond)(fn)

    for (copy, sends, _), (da, _) in zip(halos, ways):
        when(da, sends, copy.start)

    turned[:, 0 : 2 * tile_lon] = jnp.zeros((channels, 2 * tile_lon), bf16)
    turned[:, rows * tile_lon : (rows + 2) * tile_lon] = jnp.zeros((channels, 2 * tile_lon), bf16)

    def turn(p, _):
        turned[:, pl.ds(pl.multiple_of((p + 2) * tile_lon, tile_lon), tile_lon)] = feat_ref[p].T
        return 0

    lax.fori_loop(0, tile_lat, turn, 0)
    mixer[...] = jnp.zeros_like(mixer)
    for a in range(3):
        for b in range(3):
            tap = weight_ref[a, b].T
            for r in range(2):
                at = ((r + 2 - a) * 3 + b) * channels
                mixer[at : at + channels, r * channels : (r + 1) * channels] = tap
    total[...] = jnp.zeros_like(total)

    for (copy, _, takes), (da, db), ref in zip(halos, ways, landed):

        def take(copy=copy, da=da, db=db, ref=ref):
            copy.wait_recv()
            high = {-1: rows - up, 0: 0, 1: 0}[da]
            count = {-1: up, 0: rows, 1: down}[da]
            left = {-1: cols - up, 0: 0, 1: 0}[db]
            width = {-1: up, 0: cols, 1: down}[db]

            def add(i, _):
                grid[high + i, left : left + width, :] += ref[i].astype(f32)
                return 0

            lax.fori_loop(0, count, add, 0)

        when(da, takes, take)

    @pl.when(lat == 0)
    def _():
        grid[0] = jnp.zeros(grid.shape[1:], f32)

    @pl.when(lat == lat_total - 1)
    def _():
        grid[rows - 1] = jnp.zeros(grid.shape[1:], f32)

    def shift(i, _):
        at = pl.ds(pl.multiple_of(i * tile_lon, tile_lon), tile_lon)
        for b in range(3):
            windows[at, b * channels : (b + 1) * channels] = grid[
                i, 2 - b : 2 - b + tile_lon, :
            ].astype(bf16)
        return 0

    lax.fori_loop(0, rows, shift, 0)
    step = next(n for n in (11, 6, 3, 2, 1) if rows % n == 0)
    depth = step * tile_lon

    def weigh(k, _):
        start = k * depth
        lhs = jnp.concatenate(
            [
                turned[:, pl.ds(pl.multiple_of(start + a * tile_lon, tile_lon), depth)]
                for a in range(3)
            ],
            axis=0,
        )
        rhs = windows[pl.ds(pl.multiple_of(start, tile_lon), depth), :]
        total[...] += jnp.dot(lhs, rhs, preferred_element_type=f32)
        return 0

    lax.fori_loop(0, rows // step, weigh, 0)
    for a in range(3):
        for b in range(3):
            at = (a * 3 + b) * channels
            flat[at : at + channels, :] = total[
                a * channels : (a + 1) * channels, b * channels : (b + 1) * channels
            ]
    share = pieces.shape[1]

    def cut(d, _):
        pieces[d] = flat[pl.ds(d * share, share), :].astype(bf16)
        return 0

    lax.fori_loop(0, devices, cut, 0)
    part = math.gcd(tile_lat // 2, 8)
    strides = tile_lat // 2 // part
    first, second = strides // 4, strides * 3 // 4

    def apply(k, _):
        lhs = jnp.concatenate(
            [
                jnp.concatenate(
                    [
                        windows[
                            pl.ds(
                                pl.multiple_of((2 * (k * part + j) + r) * tile_lon, tile_lon),
                                tile_lon,
                            ),
                            :,
                        ]
                        for r in range(4)
                    ],
                    axis=1,
                )
                for j in range(part)
            ],
            axis=0,
        )
        acc = jnp.dot(lhs, mixer[...], preferred_element_type=f32).astype(bf16)
        for j in range(part):
            for r in range(2):
                ig_ref[2 * (k * part + j) + r] = acc[
                    j * tile_lon : (j + 1) * tile_lon, r * channels : (r + 1) * channels
                ]
        return 0

    def paired(src, dst, n):
        return pltpu.make_async_remote_copy(
            src_ref=src,
            dst_ref=dst,
            send_sem=pair_send.at[n],
            recv_sem=pair_recv.at[n],
            device_id=place(chip * 2 + other),
            device_id_type=pl.DeviceIdType.MESH,
        )

    def scattered(peer, slot):
        return pltpu.make_async_remote_copy(
            src_ref=pieces.at[core * chips + peer],
            dst_ref=parts.at[slot],
            send_sem=part_send.at[peer],
            recv_sem=part_recv.at[slot],
            device_id=place(peer * 2 + core),
            device_id_type=pl.DeviceIdType.MESH,
        )

    def shared(peer, slot):
        return pltpu.make_async_remote_copy(
            src_ref=mine,
            dst_ref=gathered.at[core * chips + slot],
            send_sem=all_send.at[peer],
            recv_sem=all_recv.at[slot],
            device_id=place(peer * 2 + core),
            device_id_type=pl.DeviceIdType.MESH,
        )

    def each(fn):
        def body(k, _):
            fn((chip + k) % chips)
            return 0

        lax.fori_loop(1, chips, body, 0)

    swap = paired(pieces.at[pl.ds(other * chips, chips)], twin, 0)
    swap.start()
    lax.fori_loop(0, first, apply, 0)
    swap.wait_recv()

    def merge(p, _):
        at = core * chips + p
        pieces[at] = (flat[pl.ds(at * share, share), :] + twin[p].astype(f32)).astype(bf16)
        return 0

    lax.fori_loop(0, chips, merge, 0)
    each(lambda peer: scattered(peer, chip).start())
    lax.fori_loop(first, second, apply, 0)
    parts[chip] = pieces[core * chips + chip]
    each(lambda peer: scattered(peer, peer).wait_recv())

    def gather_sum(p, acc):
        return acc + parts[p].astype(f32)

    mine[...] = lax.fori_loop(
        0, chips, gather_sum, jnp.zeros((share, channels), f32)
    ).astype(bf16)
    each(lambda peer: shared(peer, chip).start())
    gathered[core * chips + chip] = mine[...]
    lax.fori_loop(second, strides, apply, 0)
    each(lambda peer: shared(peer, peer).wait_recv())
    held = gathered.at[pl.ds(core * chips, chips)]
    back = paired(held, held, 1)
    back.start()

    def spill(d, _):
        wg_ref[pl.ds(d * share, share), :] = gathered[d].astype(f32)
        return 0

    lax.fori_loop(core * chips, (core + 1) * chips, spill, 0)
    back.wait_recv()
    lax.fori_loop(other * chips, (other + 1) * chips, spill, 0)
    for (copy, sends, _), (da, _) in zip(halos, ways):
        when(da, sends, copy.wait_send)
    swap.wait_send()
    back.wait_send()
    each(lambda peer: scattered(peer, chip).wait_send())
    each(lambda peer: shared(peer, chip).wait_send())


def shards(grad_rows, owner, lat_offset, lon_offset, position, live_count, features, conv_weight):
    lat_total = lax.axis_size("lat")
    lon_total = lax.axis_size("lon")
    device_total = lat_total * lon_total
    row_total, channels = grad_rows.shape
    tile_lat, tile_lon = features.shape[:2]
    capacity = max(2, 2 * row_total // device_total)
    smem = pl.BlockSpec(memory_space=pltpu.SMEM)
    vmem = pl.BlockSpec(memory_space=pltpu.VMEM)

    message = (device_total, capacity + geom_rows, channels)
    incoming = pl.pallas_call(
        functools.partial(pack_kernel, capacity, lat_total, lon_total),
        out_shape=jax.ShapeDtypeStruct(message, bf16),
        in_specs=[smem] + [vmem] * 5,
        out_specs=vmem,
        scratch_shapes=[
            pltpu.VMEM(message, bf16),
            pltpu.VMEM((device_total, channels), f32),
            pltpu.SemaphoreType.DMA((device_total,)),
            pltpu.SemaphoreType.DMA((device_total,)),
        ],
        compiler_params=pltpu.CompilerParams(
            vmem_limit_bytes=24 * 2**20, collective_id=1, has_side_effects=True
        ),
        name="pack",
    )(
        live_count,
        grad_rows,
        owner.reshape(1, row_total),
        lat_offset.reshape(1, row_total),
        lon_offset.reshape(1, row_total),
        position.T,
    )
    info = incoming[:, capacity : capacity + 5, :capacity].transpose(1, 0, 2).astype(f32)
    info = info.reshape(-1)

    rows, cols = tile_lat + 2, tile_lon + 2
    tall = tile_lat + taps - 1
    wide = -(-(tile_lon + taps - 1) // 8) * 8
    up, down = before + 1, after + 1
    lanes = math.gcd(capacity, 4)
    strip_shapes = [
        (up, cols),
        (down, cols),
        (rows, up),
        (rows, down),
        (up, up),
        (up, down),
        (down, up),
        (down, down),
    ]
    own, *strips = pl.pallas_call(
        functools.partial(scatter_kernel, capacity, lanes),
        out_shape=[
            jax.ShapeDtypeStruct(shape + (channels,), bf16)
            for shape in [(rows, cols)] + strip_shapes
        ],
        in_specs=[smem, vmem],
        out_specs=[vmem] * 9,
        scratch_shapes=[
            pltpu.VMEM((lanes, tall, wide, channels), f32),
            pltpu.VMEM((capacity, channels), f32),
        ],
        compiler_params=pltpu.CompilerParams(vmem_limit_bytes=32 * 2**20),
        name="scatter",
    )(
        info,
        incoming,
    )
    flat_rows = 9 * channels
    share = flat_rows // device_total
    ring = pltpu.VMEM((device_total, share, channels), bf16)
    half_ring = pltpu.VMEM((device_total // 2, share, channels), bf16)
    input_grad, weight_grad = pl.pallas_call(
        functools.partial(conv_kernel, lat_total, lon_total),
        out_shape=[
            jax.ShapeDtypeStruct((tile_lat, tile_lon, channels), bf16),
            jax.ShapeDtypeStruct((flat_rows, channels), f32),
        ],
        in_specs=[vmem] * 11,
        out_specs=[vmem] * 2,
        scratch_shapes=[pltpu.VMEM(shape + (channels,), bf16) for shape in strip_shapes]
        + [
            pltpu.VMEM((rows, -(-cols // 8) * 8, channels), f32),
            pltpu.VMEM((rows * tile_lon, 3 * channels), bf16),
            pltpu.VMEM((channels, (rows + 2) * tile_lon), bf16),
            pltpu.VMEM((3 * channels, 3 * channels), f32),
            pltpu.VMEM((flat_rows, channels), f32),
            pltpu.VMEM((4 * 3 * channels, 2 * channels), bf16),
            ring,
            half_ring,
            half_ring,
            pltpu.VMEM((share, channels), bf16),
            ring,
            pltpu.SemaphoreType.DMA((8,)),
            pltpu.SemaphoreType.DMA((8,)),
            pltpu.SemaphoreType.DMA((2,)),
            pltpu.SemaphoreType.DMA((2,)),
            pltpu.SemaphoreType.DMA((device_total // 2,)),
            pltpu.SemaphoreType.DMA((device_total // 2,)),
            pltpu.SemaphoreType.DMA((device_total // 2,)),
            pltpu.SemaphoreType.DMA((device_total // 2,)),
        ],
        compiler_params=pltpu.CompilerParams(
            vmem_limit_bytes=36 * 2**20, collective_id=0, has_side_effects=True
        ),
        name="conv",
    )(own, *strips, features, conv_weight)
    return input_grad, weight_grad.reshape(3, 3, channels, channels)


def solution(mesh):
    placed = (
        P(("lat", "lon"), None),
        P(("lat", "lon"), None),
        P(("lat", "lon")),
        P(("lat", "lon")),
        P(("lat", "lon"), None),
        P(("lat", "lon")),
        P("lat", "lon", None),
        P(),
    )
    return jax.shard_map(
        shards, mesh=mesh, in_specs=placed, out_specs=(P("lat", "lon", None), P()), check_vma=False
    )
```

profile of v0, /device:TPU:1, one launch (start us, length us, event | category | flops | bytes accessed | tf_op | source)
XLA Modules:
  0.0 86.9 jit_solution(7736202530238172738)
XLA Ops:
  0.6 0.0 copy-start.1
  1.3 0.0 copy-start.2
  1.3 0.9 %copy-done.2 = bf16[1024,128]{1,0:T(8,128)(2,1)S(1)} copy-done((bf16[1024,128]{1,0:T(8,128)(2,1)S(1)}, bf16[1024,128]{1,0:T(8,128)(2,1)}, u32[]{:S(2)}) %copy-start.2) | copy-done | bytes 262168
  2.3 0.0 copy-start.3
  2.3 0.7 copy-done.3
  3.0 0.0 copy-start.4
  3.0 0.7 copy-done.4
  3.7 0.0 copy-start.5
  3.7 0.7 copy-done.5
  4.3 0.0 copy-start.6
  4.3 0.7 copy-done.6
  5.0 21.4 %pack.1.msg_ref = bf16[32,72,128]{2,1,0:T(8,128)(2,1)S(1)} custom-call(s32[1]{0:T(128)S(6)} %copy.13.live_ref, bf16[1024,128]{1,0:T(8,128)(2,1)S(1)} %copy-done.2, s32[1,1024]{1,0:T(1,128)S(1)} %bitcast.8, s32[1,1024]{1,0:T(1,128)S(1)} %bitcast.9, s32[1,1024]{1,0:T(1,128)S(1)} %bitcast.10, bf16[2,1024]{1,0:T(2,128)(2,1)S(1)} %bitcast.11), custom_call_target="tpu_custom_call" | custom-call | tf_op jit(solution)/shard_map/pack/pallas_call | solution.py:508
  26.4 0.1 reshape.28.info_ref
  26.5 21.4 %scatter.1 = (bf16[66,130,128]{2,1,0:T(8,128)(2,1)S(1)}, bf16[4,130,128]{2,1,0:T(8,128)(2,1)S(1)}, bf16[5,130,128]{2,1,0:T(8,128)(2,1)S(1)}, bf16[66,4,128]{2,1,...) custom-call(f32[10240]{0:T(1024)S(1)} %reshape.28.info_ref, ...), custom_call_target="tpu_custom_call" | custom-call | tf_op jit(solution)/shard_map/scatter/pallas_call | solution.py:549
  47.9 0.0 copy-done.1
  47.9 0.0 copy-start
  48.0 1.6 %copy-done = bf16[64,128,128]{2,1,0:T(8,128)(2,1)S(1)} copy-done((bf16[64,128,128]{2,1,0:T(8,128)(2,1)S(1)}, bf16[64,128,128]{2,1,0:T(8,128)(2,1)}, u32[]{:S(2)}) %copy-start) | copy-done | bytes 2097176
  49.5 35.2 %conv.1 = (bf16[64,128,128]{2,1,0:T(8,128)(2,1)S(1)}, f32[1152,128]{1,0:T(8,128)S(1)}) custom-call(bf16[66,130,128]{2,1,0:T(8,128)(2,1)S(1)} %get-tuple-element.13.own_ref, bf16[4,130,128]{2,1,0:T(8,128)(2,1)S(1)} %get-tuple-element.14.refs_0_, bf16[5,130,128]{2,1,0:T(8,128)(2,1)S(1)} %get-tuple-element.15.refs_1_, ...), custom_call_target="tpu_custom_call" | custom-call | tf_op jit(solution)/shard_map/conv/pallas_call | solution.py:571
  84.8 1.3 %copy.14 = bf16[64,128,128]{2,1,0:T(8,128)(2,1)} copy(bf16[64,128,128]{2,1,0:T(8,128)(2,1)S(1)} %get-tuple-element.26) | data formatting | bytes 4194304
  86.1 0.8 copy.15
  (2 shorter events, 0.0 us)
Async XLA Ops:
  0.6 47.3 %copy-start.1 = (bf16[3,3,128,128]{3,2,1,0:T(8,128)(2,1)S(1)}, bf16[3,3,128,128]{3,2,1,0:T(8,128)(2,1)}, u32[]{:S(2)}) copy-start(bf16[3,3,128,128]{3,2,1,0:T(8,128)(2,1)} %refs_9_.1) | copy-start | bytes 884740
  1.3 1.0 %copy-start.2 = (bf16[1024,128]{1,0:T(8,128)(2,1)S(1)}, bf16[1024,128]{1,0:T(8,128)(2,1)}, u32[]{:S(2)}) copy-start(bf16[1024,128]{1,0:T(8,128)(2,1)} %rows_ref.1) | copy-start | bytes 786436
  2.3 0.7 copy-start.3
  3.0 0.7 copy-start.4
  3.7 0.7 copy-start.5
  4.3 0.7 copy-start.6
  47.9 1.6 %copy-start = (bf16[64,128,128]{2,1,0:T(8,128)(2,1)S(1)}, bf16[64,128,128]{2,1,0:T(8,128)(2,1)}, u32[]{:S(2)}) copy-start(bf16[64,128,128]{2,1,0:T(8,128)(2,1)} %refs_8_.1) | copy-start | bytes 6291460
where the time goes:
time: 87.2 us; the launch traced here: 86.9 us
  Pallas kernels  78 us (89%)
  local copies, waits for them, and re-layouts  7.51 us (9%)
  between operations  1.4 us (2%)
    pallas_call x1, Pallas kernels, shards(): pl.pallas_call(functools.partial(conv_kernel, lat_total, lon_total), out_...  35.2 us
    pallas_call x1, Pallas kernels, shards(): pl.pallas_call(functools.partial(scatter_kernel, capacity, lanes), out_sh...  21.4 us
    pallas_call x1, Pallas kernels, shards(): pl.pallas_call(functools.partial(pack_kernel, capacity, lat_total, lon_to...  21.4 us
    unnamed x16, local copies, waits for them, and re-layouts  7.41 us

commit v1 on v0

--- a/solution.py
+++ b/solution.py
@@ -17,28 +17,50 @@
 bf16 = jnp.bfloat16
 
 
-def pack_kernel(
+def spread_kernel(
     capacity,
     lat_total,
     lon_total,
+    tile_lat,
+    tile_lon,
     live_ref,
     rows_ref,
     owner_ref,
     lat_ref,
     lon_ref,
     pos_ref,
-    out_ref,
+    own_ref,
+    up_ref,
+    down_ref,
+    left_ref,
+    right_ref,
+    ul_ref,
+    ur_ref,
+    dl_ref,
+    dr_ref,
     held,
-    tally,
+    inbox,
+    sums,
+    canvas,
+    lat_taps,
+    lon_taps,
+    halves,
     send_sem,
     recv_sem,
 ):
-    devices = out_ref.shape[0]
+    devices = inbox.shape[0]
     row_total, channels = rows_ref.shape
-    me = lax.axis_index("lat") * lon_total + lax.axis_index("lon")
+    lat, lon = lax.axis_index("lat"), lax.axis_index("lon")
+    me = lon * lat_total + lat
+    span = halves.shape[0]
+    group = span // capacity
+    groups = devices // group
+    mine = me // group
+    half = tile_lon // 2
+    inv = 1.0 / (2.0 * rbf_scale * rbf_scale)
 
     def place(peer):
-        return (peer // lon_total, peer % lon_total)
+        return (peer % lat_total, peer // lat_total)
 
     barrier = pltpu.get_barrier_semaphore()
 
@@ -49,17 +71,30 @@
         return 0
 
     lax.fori_loop(1, devices, greet, 0)
+
     live = lax.broadcasted_iota(jnp.int32, (1, row_total), 1) < live_ref[0]
-    owner = jnp.where(live, owner_ref[...], devices)
+    tile = owner_ref[...].astype(f32)
+    tile_row = jnp.floor((tile + 0.5) * (1.0 / lon_total))
+    owner = (tile - tile_row * lon_total) * lat_total + tile_row
+    owner = jnp.where(live, owner, float(devices)).astype(jnp.int32)
     match = lax.broadcasted_iota(jnp.int32, (devices, row_total), 0) == owner
     match = jnp.where(match, 1.0, 0.0)
-    tally[...] = jnp.broadcast_to(jnp.sum(match, axis=1, keepdims=True), tally.shape)
-    upper = lax.broadcasted_iota(jnp.int32, (row_total, row_total), 0) < lax.broadcasted_iota(
-        jnp.int32, (row_total, row_total), 1
+    blocks = row_total // 128
+    upper = lax.broadcasted_iota(jnp.int32, (128, 128), 0) < lax.broadcasted_iota(
+        jnp.int32, (128, 128), 1
     )
     upper = jnp.where(upper, 1.0, 0.0).astype(bf16)
-    earlier = jnp.dot(match.astype(bf16), upper, preferred_element_type=f32)
-    rank = jnp.sum(earlier * match, axis=0, keepdims=True).astype(jnp.int32)
+    parts = [match[:, k * 128 : (k + 1) * 128] for k in range(blocks)]
+    earlier = jnp.dot(
+        jnp.concatenate(parts, axis=0).astype(bf16), upper, preferred_element_type=f32
+    )
+    before_block = jnp.zeros((devices, 1), f32)
+    ranks = []
+    for k, part in enumerate(parts):
+        ahead = earlier[k * devices : (k + 1) * devices] + before_block
+        ranks.append(jnp.sum(ahead * part, axis=0, keepdims=True))
+        before_block = before_block + jnp.sum(part, axis=1, keepdims=True)
+    rank = jnp.concatenate(ranks, axis=1).astype(jnp.int32)
     slot = owner * capacity + rank
     geometry = jnp.concatenate(
         [
@@ -70,10 +105,10 @@
         ],
         axis=0,
     ).astype(bf16)
-    group = math.gcd(devices, max(1, 256 // capacity))
-    groups = devices // group
-    line = lax.broadcasted_iota(jnp.int32, (group * capacity, row_total), 0)
-    row_line = lax.broadcasted_iota(jnp.int32, (geom_rows, capacity), 0)
+    fold = 128 // capacity
+    chunk = math.gcd(group, max(1, 256 // capacity))
+    line = lax.broadcasted_iota(jnp.int32, (chunk * capacity, row_total), 0)
+    lane_block = lax.broadcasted_iota(jnp.int32, (geom_rows, 128), 1) // capacity
 
     def build(first):
         hit = jnp.where(line == slot - first * capacity, 1.0, 0.0).astype(bf16)
@@ -81,18 +116,21 @@
         info = lax.dot_general(
             geometry, hit, (((1,), (1,)), ((), ())), preferred_element_type=f32
         )
-        for i in range(group):
+        for i in range(chunk):
             held[first + i, 0:capacity, :] = placed[i * capacity : (i + 1) * capacity]
-            held[first + i, capacity : capacity + geom_rows, 0:capacity] = jnp.where(
-                row_line == 4,
-                tally[pl.ds(first + i, 1), 0:capacity],
-                info[:, i * capacity : (i + 1) * capacity],
-            ).astype(bf16)
+        for v in range(chunk // fold):
+            piece = info[:, v * 128 : (v + 1) * 128]
+            rolled = [piece] + [pltpu.roll(piece, s * capacity, 1) for s in range(1, fold)]
+            for i in range(fold):
+                tiled = rolled[(fold - i) % fold]
+                for t in range(1, fold):
+                    tiled = jnp.where(lane_block == t, rolled[(t - i) % fold], tiled)
+                held[first + v * fold + i, capacity : capacity + geom_rows, :] = tiled.astype(bf16)
 
     def copy_to(peer, slot_at):
         return pltpu.make_async_remote_copy(
             src_ref=held.at[peer],
-            dst_ref=out_ref.at[slot_at],
+            dst_ref=inbox.at[slot_at],
             send_sem=send_sem.at[peer],
             recv_sem=recv_sem.at[slot_at],
             device_id=place(peer),
@@ -100,128 +138,110 @@
         )
 
     def send(first):
-        for i in range(group):
+        for i in range(chunk):
             peer = first + i
 
             @pl.when(peer != me)
             def _():
                 copy_to(peer, me).start()
 
-    odd = groups // 2
-
-    def first_of(k):
-        ahead = jnp.where(k < odd, 2 * k + 1, 2 * (k - odd))
-        return ((me // group + ahead) % groups) * group
-
-    build(first_of(0))
+    if groups == 4:
+        order = [3 - mine, (mine + 2) % 4, mine + 1 - 2 * (mine % 2), mine]
+    else:
+        order = [(mine + groups // 2 + k) % groups for k in range(groups)]
+    per = group // chunk
+    steps = [(q, c) for q in order for c in range(per)]
+    first_of = [q * group + c * chunk for q, c in steps]
+    build(first_of[0])
     pl.semaphore_wait(barrier, devices - 1)
-
-    def work(k, _):
-        build(first_of(k))
-        send(first_of(k - 1))
-        return 0
-
-    lax.fori_loop(1, groups, work, 0)
-    send(first_of(groups - 1))
-    out_ref[me] = held[me]
-
-    def each(fn):
-        def body(k, _):
-            fn((me + k) % devices)
+    send(first_of[0])
+    for first in first_of[1:]:
+        build(first)
+        send(first)
+    inbox[me] = held[me]
+
+    sums[...] = jnp.zeros_like(sums)
+    line_lat = lax.broadcasted_iota(jnp.int32, (lat_taps.shape[0], span), 0).astype(f32)
+    line_lon = lax.broadcasted_iota(jnp.int32, (lon_taps.shape[0], span), 0).astype(f32)
+    lanes = lax.broadcasted_iota(jnp.int32, (8, 128), 1) // capacity
+    wide = sums.shape[1]
+    deep = lon_taps.shape[0]
+    stride = 8
+
+    def taps_of(line, base, frac):
+        tap = line - base
+        d = tap - (frac + before)
+        weight = jnp.exp(-(d * d) * inv)
+        return jnp.where((tap >= 0.0) & (tap <= taps - 1.0), weight, 0.0)
+
+    def collect(q):
+        for i in range(group):
+            peer = q * group + i
+
+            @pl.when(peer != me)
+            def _():
+                copy_to(peer, peer).wait_recv()
+
+        first = q * group
+        infos = []
+        for v in range(span // 128):
+            at = first + v * fold
+            info = inbox[at, capacity : capacity + geom_rows, :].astype(f32)
+            for t in range(1, fold):
+                info = jnp.where(
+                    lanes == t, inbox[at + t, capacity : capacity + geom_rows, :].astype(f32), info
+                )
+            infos.append(info)
+        info = jnp.concatenate(infos, axis=1)
+        lat_frac, lon_frac, row_at, col_at = (info[k : k + 1] for k in range(4))
+        right = jnp.where(col_at >= half, 1.0, 0.0)
+        lat_taps[...] = taps_of(line_lat, row_at, lat_frac).astype(bf16).astype(f32)
+        lon_taps[...] = taps_of(line_lon, col_at - right * half, lon_frac).astype(bf16)
+        for v in range(span // 128):
+            side = jnp.broadcast_to(right[:, v * 128 : (v + 1) * 128], (128, 128)).T.astype(bf16)
+            rows = jnp.concatenate(
+                [inbox[first + v * fold + t, 0:capacity, :] for t in range(fold)], axis=0
+            )
+            at = slice(v * 128, (v + 1) * 128)
+            on_right = rows * side
+            halves[at, 0:channels] = rows - on_right
+            halves[at, channels : 2 * channels] = on_right
+
+        def add(k, _):
+            lhs = []
+            for j in range(stride):
+                row = jnp.broadcast_to(lat_taps[pl.ds(k * stride + j, 1), :], (16, span)).astype(bf16)
+                for t in range(deep // 16):
+                    lhs.append(row * lon_taps[t * 16 : (t + 1) * 16, :])
+            out = jnp.dot(jnp.concatenate(lhs, axis=0), halves[...], preferred_element_type=f32)
+            for j in range(stride):
+                sums[k * stride + j] += out[j * deep : j * deep + wide]
             return 0
 
-        lax.fori_loop(1, devices, body, 0)
-
-    each(lambda peer: copy_to(peer, peer).wait_recv())
-    each(lambda peer: copy_to(peer, me).wait_send())
-
-
-def scatter_kernel(
-    capacity,
-    lanes,
-    info_ref,
-    msg_ref,
-    own_ref,
-    up_ref,
-    down_ref,
-    left_ref,
-    right_ref,
-    ul_ref,
-    ur_ref,
-    dl_ref,
-    dr_ref,
-    canvas,
-    block,
-):
-    sources = msg_ref.shape[0]
-    slots = sources * capacity
+        lax.fori_loop(0, sums.shape[0] // stride, add, 0)
+
+    for q in order[::-1]:
+        collect(q)
+
     rows, cols = own_ref.shape[0], own_ref.shape[1]
-    tall = canvas.shape[1]
-    inv = 1.0 / (2.0 * rbf_scale * rbf_scale)
-
-    def clear(i, _):
-        for j in range(lanes):
-            canvas[j, i] = jnp.zeros(canvas.shape[2:], f32)
-        return 0
-
-    lax.fori_loop(0, tall, clear, 0)
-    line = lax.broadcasted_iota(jnp.int32, (taps, canvas.shape[3]), 0).astype(f32) - before
-    level = [math.exp(-((a - before) ** 2 - before**2) * inv) for a in range(taps)]
-
-    def source(src, _):
-        block[...] = msg_ref[src, 0:capacity, :].astype(f32)
-
-        def prepare(i):
-            terms = []
-            for j in range(lanes):
-                s = i * lanes + j
-                at = src * capacity + s
-                fa, fb = info_ref[at], info_ref[at + slots]
-                d = line - fb
-                t = jnp.exp(-(d * d + (before + fa) * (before + fa)) * inv) * block[pl.ds(s, 1), :]
-                g = jnp.exp(jnp.full(t.shape, 2.0 * inv, f32) * fa)
-                r = info_ref[at + 2 * slots].astype(jnp.int32)
-                c = info_ref[at + 3 * slots].astype(jnp.int32)
-                terms.append((r, c, t, g))
-            return tuple(terms)
-
-        trips = (info_ref[4 * slots + src * capacity].astype(jnp.int32) + lanes - 1) // lanes
-
-        def step(i, terms):
-            ahead = prepare(jnp.minimum(i + 1, trips - 1))
-            sums = []
-            for j, (r, c, t, g) in enumerate(terms):
-                for a in range(taps):
-                    sums.append(canvas[j, r + a, pl.ds(c, taps), :] + t * level[a])
-                    t = t * g
-            for j, (r, c, _, _) in enumerate(terms):
-                for a in range(taps):
-                    canvas[j, r + a, pl.ds(c, taps), :] = sums[j * taps + a]
-            return ahead
-
-        lax.fori_loop(0, trips, step, prepare(0))
-        return 0
-
-    lax.fori_loop(0, sources, source, 0)
+    tall = canvas.shape[0]
+
+    def join(i, _):
+        canvas[i, 0:half, :] = sums[i, 0:half, 0:channels]
+        canvas[i, half:wide, :] = (
+            sums[i, half:wide, 0:channels] + sums[i, 0 : wide - half, channels : 2 * channels]
+        )
+        canvas[i, wide : wide + half, :] = sums[i, wide - half : wide, channels : 2 * channels]
+        return 0
+
+    lax.fori_loop(0, tall, join, 0)
     up, down = before + 1, after + 1
     inset = before - 1
 
-    def total(i):
-        whole = canvas[0, i]
-        for j in range(1, lanes):
-            whole = whole + canvas[j, i]
-        canvas[0, i] = whole
-
-    def finish(i, _):
-        total(i)
-        return 0
-
-    lax.fori_loop(0, tall, finish, 0)
-
     def emit(i, _):
-        own_ref[i] = canvas[0, i + inset, inset : inset + cols, :].astype(bf16)
-        left_ref[i] = canvas[0, i + inset, 0:up, :].astype(bf16)
-        right_ref[i] = canvas[0, i + inset, inset + cols - 2 : inset + cols - 2 + down, :].astype(bf16)
+        own_ref[i] = canvas[i + inset, inset : inset + cols, :].astype(bf16)
+        left_ref[i] = canvas[i + inset, 0:up, :].astype(bf16)
+        right_ref[i] = canvas[i + inset, inset + cols - 2 : inset + cols - 2 + down, :].astype(bf16)
         return 0
 
     lax.fori_loop(0, rows, emit, 0)
@@ -232,7 +252,16 @@
     ):
         for i in range(count):
             for (start, width), ref in zip(spans, refs):
-                ref[i] = canvas[0, first + i, start : start + width, :].astype(bf16)
+                ref[i] = canvas[first + i, start : start + width, :].astype(bf16)
+
+    def each(fn):
+        def body(k, _):
+            fn((me + k) % devices)
+            return 0
+
+        lax.fori_loop(1, devices, body, 0)
+
+    each(lambda peer: copy_to(peer, me).wait_send())
 
 
 def conv_kernel(
@@ -504,38 +533,11 @@
     smem = pl.BlockSpec(memory_space=pltpu.SMEM)
     vmem = pl.BlockSpec(memory_space=pltpu.VMEM)
 
-    message = (device_total, capacity + geom_rows, channels)
-    incoming = pl.pallas_call(
-        functools.partial(pack_kernel, capacity, lat_total, lon_total),
-        out_shape=jax.ShapeDtypeStruct(message, bf16),
-        in_specs=[smem] + [vmem] * 5,
-        out_specs=vmem,
-        scratch_shapes=[
-            pltpu.VMEM(message, bf16),
-            pltpu.VMEM((device_total, channels), f32),
-            pltpu.SemaphoreType.DMA((device_total,)),
-            pltpu.SemaphoreType.DMA((device_total,)),
-        ],
-        compiler_params=pltpu.CompilerParams(
-            vmem_limit_bytes=24 * 2**20, collective_id=1, has_side_effects=True
-        ),
-        name="pack",
-    )(
-        live_count,
-        grad_rows,
-        owner.reshape(1, row_total),
-        lat_offset.reshape(1, row_total),
-        lon_offset.reshape(1, row_total),
-        position.T,
-    )
-    info = incoming[:, capacity : capacity + 5, :capacity].transpose(1, 0, 2).astype(f32)
-    info = info.reshape(-1)
-
     rows, cols = tile_lat + 2, tile_lon + 2
-    tall = tile_lat + taps - 1
-    wide = -(-(tile_lon + taps - 1) // 8) * 8
+    tall = -(-(tile_lat + taps - 1) // 8) * 8
+    wide = tile_lon // 2 + 8
+    span = math.gcd(device_total, max(1, 512 // capacity)) * capacity
     up, down = before + 1, after + 1
-    lanes = math.gcd(capacity, 4)
     strip_shapes = [
         (up, cols),
         (down, cols),
@@ -546,23 +548,37 @@
         (down, up),
         (down, down),
     ]
+    message = (device_total, capacity + geom_rows, channels)
     own, *strips = pl.pallas_call(
-        functools.partial(scatter_kernel, capacity, lanes),
+        functools.partial(spread_kernel, capacity, lat_total, lon_total, tile_lat, tile_lon),
         out_shape=[
             jax.ShapeDtypeStruct(shape + (channels,), bf16)
             for shape in [(rows, cols)] + strip_shapes
         ],
-        in_specs=[smem, vmem],
+        in_specs=[smem] + [vmem] * 5,
         out_specs=[vmem] * 9,
         scratch_shapes=[
-            pltpu.VMEM((lanes, tall, wide, channels), f32),
-            pltpu.VMEM((capacity, channels), f32),
+            pltpu.VMEM(message, bf16),
+            pltpu.VMEM(message, bf16),
+            pltpu.VMEM((tall, wide, 2 * channels), f32),
+            pltpu.VMEM((tall, wide + tile_lon // 2, channels), f32),
+            pltpu.VMEM((tall, span), f32),
+            pltpu.VMEM((-(-wide // 16) * 16, span), bf16),
+            pltpu.VMEM((span, 2 * channels), bf16),
+            pltpu.SemaphoreType.DMA((device_total,)),
+            pltpu.SemaphoreType.DMA((device_total,)),
         ],
-        compiler_params=pltpu.CompilerParams(vmem_limit_bytes=32 * 2**20),
-        name="scatter",
+        compiler_params=pltpu.CompilerParams(
+            vmem_limit_bytes=40 * 2**20, collective_id=1, has_side_effects=True
+        ),
+        name="spread",
     )(
-        info,
-        incoming,
+        live_count,
+        grad_rows,
+        owner.reshape(1, row_total),
+        lat_offset.reshape(1, row_total),
+        lon_offset.reshape(1, row_total),
+        position.T,
     )
     flat_rows = 9 * channels
     share = flat_rows // device_total

time: 87.2 us -> 74.7 us (0.86)
  Pallas kernels: 78 us -> 64.7 us
    pallas_call x2 -> x1, Pallas kernels: 42.8 us -> 29.4 us  [shards(): pl.pallas_call(functools.partial(spread_kernel, capacity, lat_total, lon_...]
    unnamed x16, local copies, waits for them, and re-layouts: 7.41 us -> 8.37 us
where the time goes in v1:
time: 74.7 us; the launch traced here: 74.4 us
  Pallas kernels  64.7 us (87%)
  local copies, waits for them, and re-layouts  8.37 us (11%)
  between operations  1.32 us (2%)
    pallas_call x1, Pallas kernels, shards(): pl.pallas_call(functools.partial(conv_kernel, lat_total, lon_total), out_...  35.3 us
    pallas_call x1, Pallas kernels, shards(): pl.pallas_call(functools.partial(spread_kernel, capacity, lat_total, lon_...  29.4 us
    unnamed x16, local copies, waits for them, and re-layouts  8.37 us

profile of v1, /device:TPU:1, one launch (start us, length us, event | category | flops | bytes accessed | tf_op | source)
XLA Modules:
  0.0 74.4 jit_solution(2880314276717613387)
XLA Ops:
  1.3 0.0 copy-start.2
  1.3 0.9 %copy-done.2 = bf16[1024,128]{1,0:T(8,128)(2,1)S(1)} copy-done((bf16[1024,128]{1,0:T(8,128)(2,1)S(1)}, bf16[1024,128]{1,0:T(8,128)(2,1)}, u32[]{:S(2)}) %copy-start.2) | copy-done | bytes 262168
  2.2 0.0 copy-start.3
  2.2 0.7 copy-done.3
  2.9 0.0 copy-start.4
  2.9 0.7 copy-done.4
  3.6 0.0 copy-start.5
  3.6 0.7 copy-done.5
  4.3 0.0 copy-start.6
  4.3 0.7 copy-done.6
  5.0 29.4 %spread.1 = (bf16[66,130,128]{2,1,0:T(8,128)(2,1)S(1)}, bf16[4,130,128]{2,1,0:T(8,128)(2,1)S(1)}, bf16[5,130,128]{2,1,0:T(8,128)(2,1)S(1)}, bf16[66,4,128]{2,1,0...) custom-call(s32[1]{0:T(128)S(6)} %copy.12.live_ref, ...), custom_call_target="tpu_custom_call" | custom-call | tf_op jit(solution)/shard_map/spread/pallas_call | solution.py:552
  34.4 0.0 copy-start
  34.4 1.6 %copy-done = bf16[64,128,128]{2,1,0:T(8,128)(2,1)S(1)} copy-done((bf16[64,128,128]{2,1,0:T(8,128)(2,1)S(1)}, bf16[64,128,128]{2,1,0:T(8,128)(2,1)}, u32[]{:S(2)}) %copy-start) | copy-done | bytes 2097176
  36.0 0.0 copy-start.1
  36.0 1.0 %copy-done.1 = bf16[3,3,128,128]{3,2,1,0:T(8,128)(2,1)S(1)} copy-done((bf16[3,3,128,128]{3,2,1,0:T(8,128)(2,1)S(1)}, bf16[3,3,128,128]{3,2,1,0:T(8,128)(2,1)}, u32[]{:S(2)}) %copy-start.1) | copy-done | bytes 294936
  36.9 35.3 %conv.1 = (bf16[64,128,128]{2,1,0:T(8,128)(2,1)S(1)}, f32[1152,128]{1,0:T(8,128)S(1)}) custom-call(bf16[66,130,128]{2,1,0:T(8,128)(2,1)S(1)} %get-tuple-element.13.own_ref, bf16[4,130,128]{2,1,0:T(8,128)(2,1)S(1)} %get-tuple-element.14.refs_0_, bf16[5,130,128]{2,1,0:T(8,128)(2,1)S(1)} %get-tuple-element.15.refs_1_, ...), custom_call_target="tpu_custom_call" | custom-call | tf_op jit(solution)/shard_map/conv/pallas_call | solution.py:587
  72.2 1.3 %copy.13 = bf16[64,128,128]{2,1,0:T(8,128)(2,1)} copy(bf16[64,128,128]{2,1,0:T(8,128)(2,1)S(1)} %get-tuple-element.26) | data formatting | bytes 4194304
  73.6 0.8 %copy.14 = f32[3,3,128,128]{3,2,1,0:T(8,128)} copy(f32[3,3,128,128]{3,2,1,0:T(8,128)S(1)} %bitcast.5) | data formatting | bytes 1179648
Async XLA Ops:
  1.3 1.0 %copy-start.2 = (bf16[1024,128]{1,0:T(8,128)(2,1)S(1)}, bf16[1024,128]{1,0:T(8,128)(2,1)}, u32[]{:S(2)}) copy-start(bf16[1024,128]{1,0:T(8,128)(2,1)} %rows_ref.1) | copy-start | bytes 786436
  2.2 0.7 copy-start.3
  2.9 0.7 copy-start.4
  3.6 0.7 copy-start.5
  4.3 0.7 copy-start.6
  34.4 1.6 %copy-start = (bf16[64,128,128]{2,1,0:T(8,128)(2,1)S(1)}, bf16[64,128,128]{2,1,0:T(8,128)(2,1)}, u32[]{:S(2)}) copy-start(bf16[64,128,128]{2,1,0:T(8,128)(2,1)} %refs_8_.1) | copy-start | bytes 6291460
  36.0 1.0 %copy-start.1 = (bf16[3,3,128,128]{3,2,1,0:T(8,128)(2,1)S(1)}, bf16[3,3,128,128]{3,2,1,0:T(8,128)(2,1)}, u32[]{:S(2)}) copy-start(bf16[3,3,128,128]{3,2,1,0:T(8,128)(2,1)} %refs_9_.1) | copy-start | bytes 884740

commit v2 on v1

--- a/solution.py
+++ b/solution.py
@@ -17,45 +17,37 @@
 bf16 = jnp.bfloat16
 
 
-def spread_kernel(
+def solve_kernel(
     capacity,
     lat_total,
     lon_total,
-    tile_lat,
-    tile_lon,
     live_ref,
-    rows_ref,
-    owner_ref,
-    lat_ref,
-    lon_ref,
-    pos_ref,
-    own_ref,
-    up_ref,
-    down_ref,
-    left_ref,
-    right_ref,
-    ul_ref,
-    ur_ref,
-    dl_ref,
-    dr_ref,
-    held,
-    inbox,
-    sums,
-    canvas,
-    lat_taps,
-    lon_taps,
-    halves,
-    send_sem,
-    recv_sem,
+    rows_hbm,
+    owner_hbm,
+    lat_hbm,
+    lon_hbm,
+    pos_hbm,
+    feat_hbm,
+    weight_hbm,
+    ig_ref,
+    wg_ref,
+    *refs,
 ):
+    (rows_ref, owner_ref, lat_ref, lon_ref, pos_ref, feat_ref, weight_ref) = refs[:7]
+    (held, inbox, sums, canvas, lat_taps, lon_taps, halves) = refs[7:14]
+    strips, landed = refs[14:22], refs[22:30]
+    (windows, turned, total, flat, mixer, pieces, twin, parts, mine, gathered) = refs[30:40]
+    (load_sem, send_sem, recv_sem) = refs[40:43]
+    halo_send, halo_recv, pair_send, pair_recv, part_send, part_recv, all_send, all_recv = refs[43:]
     devices = inbox.shape[0]
     row_total, channels = rows_ref.shape
+    tile_lat, tile_lon = feat_ref.shape[:2]
     lat, lon = lax.axis_index("lat"), lax.axis_index("lon")
     me = lon * lat_total + lat
     span = halves.shape[0]
     group = span // capacity
     groups = devices // group
-    mine = me // group
+    ours = me // group
     half = tile_lon // 2
     inv = 1.0 / (2.0 * rbf_scale * rbf_scale)
 
@@ -70,7 +62,26 @@
         )
         return 0
 
+    loads = [
+        pltpu.make_async_copy(src, dst, load_sem.at[k])
+        for k, (src, dst) in enumerate(
+            zip(
+                (rows_hbm, owner_hbm, lat_hbm, lon_hbm, pos_hbm, feat_hbm, weight_hbm),
+                (rows_ref, owner_ref, lat_ref, lon_ref, pos_ref, feat_ref, weight_ref),
+            )
+        )
+    ]
+    for load in loads:
+        load.start()
     lax.fori_loop(1, devices, greet, 0)
+    sums[...] = jnp.zeros_like(sums)
+    mixer[...] = jnp.zeros_like(mixer)
+    total[...] = jnp.zeros_like(total)
+    rows, cols = tile_lat + 2, tile_lon + 2
+    turned[:, 0 : 2 * tile_lon] = jnp.zeros((channels, 2 * tile_lon), bf16)
+    turned[:, rows * tile_lon : (rows + 2) * tile_lon] = jnp.zeros((channels, 2 * tile_lon), bf16)
+    for load in loads[:5]:
+        load.wait()
 
     live = lax.broadcasted_iota(jnp.int32, (1, row_total), 1) < live_ref[0]
     tile = owner_ref[...].astype(f32)
@@ -84,13 +95,13 @@
         jnp.int32, (128, 128), 1
     )
     upper = jnp.where(upper, 1.0, 0.0).astype(bf16)
-    parts = [match[:, k * 128 : (k + 1) * 128] for k in range(blocks)]
+    columns = [match[:, k * 128 : (k + 1) * 128] for k in range(blocks)]
     earlier = jnp.dot(
-        jnp.concatenate(parts, axis=0).astype(bf16), upper, preferred_element_type=f32
+        jnp.concatenate(columns, axis=0).astype(bf16), upper, preferred_element_type=f32
     )
     before_block = jnp.zeros((devices, 1), f32)
     ranks = []
-    for k, part in enumerate(parts):
+    for k, part in enumerate(columns):
         ahead = earlier[k * devices : (k + 1) * devices] + before_block
         ranks.append(jnp.sum(ahead * part, axis=0, keepdims=True))
         before_block = before_block + jnp.sum(part, axis=1, keepdims=True)
@@ -146,9 +157,9 @@
                 copy_to(peer, me).start()
 
     if groups == 4:
-        order = [3 - mine, (mine + 2) % 4, mine + 1 - 2 * (mine % 2), mine]
+        order = [3 - ours, (ours + 2) % 4, ours + 1 - 2 * (ours % 2), ours]
     else:
-        order = [(mine + groups // 2 + k) % groups for k in range(groups)]
+        order = [(ours + groups // 2 + k) % groups for k in range(groups)]
     per = group // chunk
     steps = [(q, c) for q in order for c in range(per)]
     first_of = [q * group + c * chunk for q, c in steps]
@@ -160,7 +171,21 @@
         send(first)
     inbox[me] = held[me]
 
-    sums[...] = jnp.zeros_like(sums)
+    loads[5].wait()
+
+    def turn(p, _):
+        turned[:, pl.ds(pl.multiple_of((p + 2) * tile_lon, tile_lon), tile_lon)] = feat_ref[p].T
+        return 0
+
+    lax.fori_loop(0, tile_lat, turn, 0)
+    loads[6].wait()
+    for a in range(3):
+        for b in range(3):
+            tap = weight_ref[a, b].T
+            for r in range(2):
+                at = ((r + 2 - a) * 3 + b) * channels
+                mixer[at : at + channels, r * channels : (r + 1) * channels] = tap
+
     line_lat = lax.broadcasted_iota(jnp.int32, (lat_taps.shape[0], span), 0).astype(f32)
     line_lon = lax.broadcasted_iota(jnp.int32, (lon_taps.shape[0], span), 0).astype(f32)
     lanes = lax.broadcasted_iota(jnp.int32, (8, 128), 1) // capacity
@@ -223,7 +248,6 @@
     for q in order[::-1]:
         collect(q)
 
-    rows, cols = own_ref.shape[0], own_ref.shape[1]
     tall = canvas.shape[0]
 
     def join(i, _):
@@ -237,74 +261,31 @@
     lax.fori_loop(0, tall, join, 0)
     up, down = before + 1, after + 1
     inset = before - 1
-
-    def emit(i, _):
-        own_ref[i] = canvas[i + inset, inset : inset + cols, :].astype(bf16)
-        left_ref[i] = canvas[i + inset, 0:up, :].astype(bf16)
-        right_ref[i] = canvas[i + inset, inset + cols - 2 : inset + cols - 2 + down, :].astype(bf16)
-        return 0
-
-    lax.fori_loop(0, rows, emit, 0)
     spans = ((0, up), (inset, cols), (inset + cols - 2, down))
     for count, first, refs in (
-        (up, 0, (ul_ref, up_ref, ur_ref)),
-        (down, inset + rows - 2, (dl_ref, down_ref, dr_ref)),
+        (up, 0, (strips[4], strips[0], strips[5])),
+        (down, inset + rows - 2, (strips[6], strips[1], strips[7])),
     ):
         for i in range(count):
             for (start, width), ref in zip(spans, refs):
                 ref[i] = canvas[first + i, start : start + width, :].astype(bf16)
 
-    def each(fn):
-        def body(k, _):
-            fn((me + k) % devices)
-            return 0
-
-        lax.fori_loop(1, devices, body, 0)
-
-    each(lambda peer: copy_to(peer, me).wait_send())
-
-
-def conv_kernel(
-    lat_total,
-    lon_total,
-    own_ref,
-    *refs,
-):
-    strips, (feat_ref, weight_ref, ig_ref, wg_ref) = refs[:8], refs[8:12]
-    landed = refs[12:20]
-    (grid, windows, turned, total, flat, mixer, pieces, twin, parts, mine, gathered) = refs[20:31]
-    halo_send, halo_recv, pair_send, pair_recv, part_send, part_recv, all_send, all_recv = refs[31:]
-    rows, cols = own_ref.shape[0], own_ref.shape[1]
-    tile_lat, tile_lon, channels = feat_ref.shape
-    up, down = before + 1, after + 1
-    devices = lat_total * lon_total
-    lat, lon = lax.axis_index("lat"), lax.axis_index("lon")
-    me = lat * lon_total + lon
+    def emit(i, _):
+        strips[2][i] = canvas[i + inset, 0:up, :].astype(bf16)
+        strips[3][i] = canvas[i + inset, inset + cols - 2 : inset + cols - 2 + down, :].astype(bf16)
+        return 0
+
+    lax.fori_loop(0, rows, emit, 0)
+
+    ways = ((-1, 0), (1, 0), (0, -1), (0, 1), (-1, -1), (-1, 1), (1, -1), (1, 1))
     chips = devices // 2
-    core, chip = me % 2, me // 2
+    at = lat * lon_total + lon
+    core, chip = at % 2, at // 2
     other = 1 - core
 
-    def place(peer):
+    def seat(peer):
         return (peer // lon_total, peer % lon_total)
 
-    barrier = pltpu.get_barrier_semaphore()
-
-    def greet(k, _):
-        pl.semaphore_signal(
-            barrier, inc=1, device_id=place((me + k) % devices), device_id_type=pl.DeviceIdType.MESH
-        )
-        return 0
-
-    lax.fori_loop(1, devices, greet, 0)
-
-    def fill(i, _):
-        grid[i, 0:cols, :] = own_ref[i].astype(f32)
-        return 0
-
-    lax.fori_loop(0, rows, fill, 0)
-    pl.semaphore_wait(barrier, devices - 1)
-
-    ways = ((-1, 0), (1, 0), (0, -1), (0, 1), (-1, -1), (-1, 1), (1, -1), (1, 1))
     halos = []
     for w, (da, db) in enumerate(ways):
         copy = pltpu.make_async_remote_copy(
@@ -328,23 +309,6 @@
     for (copy, sends, _), (da, _) in zip(halos, ways):
         when(da, sends, copy.start)
 
-    turned[:, 0 : 2 * tile_lon] = jnp.zeros((channels, 2 * tile_lon), bf16)
-    turned[:, rows * tile_lon : (rows + 2) * tile_lon] = jnp.zeros((channels, 2 * tile_lon), bf16)
-
-    def turn(p, _):
-        turned[:, pl.ds(pl.multiple_of((p + 2) * tile_lon, tile_lon), tile_lon)] = feat_ref[p].T
-        return 0
-
-    lax.fori_loop(0, tile_lat, turn, 0)
-    mixer[...] = jnp.zeros_like(mixer)
-    for a in range(3):
-        for b in range(3):
-            tap = weight_ref[a, b].T
-            for r in range(2):
-                at = ((r + 2 - a) * 3 + b) * channels
-                mixer[at : at + channels, r * channels : (r + 1) * channels] = tap
-    total[...] = jnp.zeros_like(total)
-
     for (copy, _, takes), (da, db), ref in zip(halos, ways, landed):
 
         def take(copy=copy, da=da, db=db, ref=ref):
@@ -355,7 +319,7 @@
             width = {-1: up, 0: cols, 1: down}[db]
 
             def add(i, _):
-                grid[high + i, left : left + width, :] += ref[i].astype(f32)
+                canvas[inset + high + i, inset + left : inset + left + width, :] += ref[i].astype(f32)
                 return 0
 
             lax.fori_loop(0, count, add, 0)
@@ -364,17 +328,17 @@
 
     @pl.when(lat == 0)
     def _():
-        grid[0] = jnp.zeros(grid.shape[1:], f32)
+        canvas[inset] = jnp.zeros(canvas.shape[1:], f32)
 
     @pl.when(lat == lat_total - 1)
     def _():
-        grid[rows - 1] = jnp.zeros(grid.shape[1:], f32)
+        canvas[inset + rows - 1] = jnp.zeros(canvas.shape[1:], f32)
 
     def shift(i, _):
         at = pl.ds(pl.multiple_of(i * tile_lon, tile_lon), tile_lon)
         for b in range(3):
-            windows[at, b * channels : (b + 1) * channels] = grid[
-                i, 2 - b : 2 - b + tile_lon, :
+            windows[at, b * channels : (b + 1) * channels] = canvas[
+                i + inset, inset + 2 - b : inset + 2 - b + tile_lon, :
             ].astype(bf16)
         return 0
 
@@ -447,7 +411,7 @@
             dst_ref=dst,
             send_sem=pair_send.at[n],
             recv_sem=pair_recv.at[n],
-            device_id=place(chip * 2 + other),
+            device_id=seat(chip * 2 + other),
             device_id_type=pl.DeviceIdType.MESH,
         )
 
@@ -457,7 +421,7 @@
             dst_ref=parts.at[slot],
             send_sem=part_send.at[peer],
             recv_sem=part_recv.at[slot],
-            device_id=place(peer * 2 + core),
+            device_id=seat(peer * 2 + core),
             device_id_type=pl.DeviceIdType.MESH,
         )
 
@@ -467,11 +431,11 @@
             dst_ref=gathered.at[core * chips + slot],
             send_sem=all_send.at[peer],
             recv_sem=all_recv.at[slot],
-            device_id=place(peer * 2 + core),
+            device_id=seat(peer * 2 + core),
             device_id_type=pl.DeviceIdType.MESH,
         )
 
-    def each(fn):
+    def each_chip(fn):
         def body(k, _):
             fn((chip + k) % chips)
             return 0
@@ -489,10 +453,10 @@
         return 0
 
     lax.fori_loop(0, chips, merge, 0)
-    each(lambda peer: scattered(peer, chip).start())
+    each_chip(lambda peer: scattered(peer, chip).start())
     lax.fori_loop(first, second, apply, 0)
     parts[chip] = pieces[core * chips + chip]
-    each(lambda peer: scattered(peer, peer).wait_recv())
+    each_chip(lambda peer: scattered(peer, peer).wait_recv())
 
     def gather_sum(p, acc):
         return acc + parts[p].astype(f32)
@@ -500,12 +464,12 @@
     mine[...] = lax.fori_loop(
         0, chips, gather_sum, jnp.zeros((share, channels), f32)
     ).astype(bf16)
-    each(lambda peer: shared(peer, chip).start())
+    each_chip(lambda peer: shared(peer, chip).start())
     gathered[core * chips + chip] = mine[...]
     lax.fori_loop(second, strides, apply, 0)
-    each(lambda peer: shared(peer, peer).wait_recv())
-    held = gathered.at[pl.ds(core * chips, chips)]
-    back = paired(held, held, 1)
+    each_chip(lambda peer: shared(peer, peer).wait_recv())
+    kept = gathered.at[pl.ds(core * chips, chips)]
+    back = paired(kept, kept, 1)
     back.start()
 
     def spill(d, _):
@@ -519,8 +483,17 @@
         when(da, sends, copy.wait_send)
     swap.wait_send()
     back.wait_send()
-    each(lambda peer: scattered(peer, chip).wait_send())
-    each(lambda peer: shared(peer, chip).wait_send())
+    each_chip(lambda peer: scattered(peer, chip).wait_send())
+    each_chip(lambda peer: shared(peer, chip).wait_send())
+
+    def each(fn):
+        def body(k, _):
+            fn((me + k) % devices)
+            return 0
+
+        lax.fori_loop(1, devices, body, 0)
+
+    each(lambda peer: copy_to(peer, me).wait_send())
 
 
 def shards(grad_rows, owner, lat_offset, lon_offset, position, live_count, features, conv_weight):
@@ -549,15 +522,31 @@
         (down, down),
     ]
     message = (device_total, capacity + geom_rows, channels)
-    own, *strips = pl.pallas_call(
-        functools.partial(spread_kernel, capacity, lat_total, lon_total, tile_lat, tile_lon),
+    flat_rows = 9 * channels
+    share = flat_rows // device_total
+    ring = pltpu.VMEM((device_total, share, channels), bf16)
+    half_ring = pltpu.VMEM((device_total // 2, share, channels), bf16)
+    dma = pltpu.SemaphoreType.DMA
+    places = [pltpu.VMEM(shape + (channels,), bf16) for shape in strip_shapes]
+    operands = (
+        grad_rows,
+        owner.reshape(1, row_total),
+        lat_offset.reshape(1, row_total),
+        lon_offset.reshape(1, row_total),
+        position.T,
+        features,
+        conv_weight,
+    )
+    input_grad, weight_grad = pl.pallas_call(
+        functools.partial(solve_kernel, capacity, lat_total, lon_total),
         out_shape=[
-            jax.ShapeDtypeStruct(shape + (channels,), bf16)
-            for shape in [(rows, cols)] + strip_shapes
+            jax.ShapeDtypeStruct((tile_lat, tile_lon, channels), bf16),
+            jax.ShapeDtypeStruct((flat_rows, channels), f32),
         ],
-        in_specs=[smem] + [vmem] * 5,
-        out_specs=[vmem] * 9,
-        scratch_shapes=[
+        in_specs=[smem] + [pl.BlockSpec(memory_space=pltpu.HBM)] * 7,
+        out_specs=[vmem] * 2,
+        scratch_shapes=[pltpu.VMEM(x.shape, x.dtype) for x in operands]
+        + [
             pltpu.VMEM(message, bf16),
             pltpu.VMEM(message, bf16),
             pltpu.VMEM((tall, wide, 2 * channels), f32),
@@ -565,36 +554,10 @@
             pltpu.VMEM((tall, span), f32),
             pltpu.VMEM((-(-wide // 16) * 16, span), bf16),
             pltpu.VMEM((span, 2 * channels), bf16),
-            pltpu.SemaphoreType.DMA((device_total,)),
-            pltpu.SemaphoreType.DMA((device_total,)),
-        ],
-        compiler_params=pltpu.CompilerParams(
-            vmem_limit_bytes=40 * 2**20, collective_id=1, has_side_effects=True
-        ),
-        name="spread",
-    )(
-        live_count,
-        grad_rows,
-        owner.reshape(1, row_total),
-        lat_offset.reshape(1, row_total),
-        lon_offset.reshape(1, row_total),
-        position.T,
-    )
-    flat_rows = 9 * channels
-    share = flat_rows // device_total
-    ring = pltpu.VMEM((device_total, share, channels), bf16)
-    half_ring = pltpu.VMEM((device_total // 2, share, channels), bf16)
-    input_grad, weight_grad = pl.pallas_call(
-        functools.partial(conv_kernel, lat_total, lon_total),
-        out_shape=[
-            jax.ShapeDtypeStruct((tile_lat, tile_lon, channels), bf16),
-            jax.ShapeDtypeStruct((flat_rows, channels), f32),
-        ],
-        in_specs=[vmem] * 11,
-        out_specs=[vmem] * 2,
-        scratch_shapes=[pltpu.VMEM(shape + (channels,), bf16) for shape in strip_shapes]
+        ]
+        + places
+        + places
         + [
-            pltpu.VMEM((rows, -(-cols // 8) * 8, channels), f32),
             pltpu.VMEM((rows * tile_lon, 3 * channels), bf16),
             pltpu.VMEM((channels, (rows + 2) * tile_lon), bf16),
             pltpu.VMEM((3 * channels, 3 * channels), f32),
@@ -605,20 +568,23 @@
             half_ring,
             pltpu.VMEM((share, channels), bf16),
             ring,
-            pltpu.SemaphoreType.DMA((8,)),
-            pltpu.SemaphoreType.DMA((8,)),
-            pltpu.SemaphoreType.DMA((2,)),
-            pltpu.SemaphoreType.DMA((2,)),
-            pltpu.SemaphoreType.DMA((device_total // 2,)),
-            pltpu.SemaphoreType.DMA((device_total // 2,)),
-            pltpu.SemaphoreType.DMA((device_total // 2,)),
-            pltpu.SemaphoreType.DMA((device_total // 2,)),
+            dma((7,)),
+            dma((device_total,)),
+            dma((device_total,)),
+            dma((8,)),
+            dma((8,)),
+            dma((2,)),
+            dma((2,)),
+            dma((device_total // 2,)),
+            dma((device_total // 2,)),
+            dma((device_total // 2,)),
+            dma((device_total // 2,)),
         ],
         compiler_params=pltpu.CompilerParams(
-            vmem_limit_bytes=36 * 2**20, collective_id=0, has_side_effects=True
+            vmem_limit_bytes=44 * 2**20, collective_id=0, has_side_effects=True
         ),
-        name="conv",
-    )(own, *strips, features, conv_weight)
+        name="solve",
+    )(live_count, *[pltpu.with_memory_space_constraint(x, pltpu.HBM) for x in operands])
     return input_grad, weight_grad.reshape(3, 3, channels, channels)
 
 

time: 74.7 us -> 65.9 us (0.88)
  local copies, waits for them, and re-layouts: 8.37 us -> 2.14 us
  Pallas kernels: 64.7 us -> 62.3 us
    unnamed x16 -> x2, local copies, waits for them, and re-layouts: 8.37 us -> 2.14 us
    pallas_call x2 -> x1, Pallas kernels: 64.7 us -> 62.3 us  [shards(): pl.pallas_call(functools.partial(solve_kernel, capacity, lat_total, lon_t...]
where the time goes in v2:
time: 65.9 us; the launch traced here: 65.7 us
  Pallas kernels  62.3 us (95%)
  local copies, waits for them, and re-layouts  2.14 us (3%)
  between operations  1.29 us (2%)
    pallas_call x1, Pallas kernels, shards(): pl.pallas_call(functools.partial(solve_kernel, capacity, lat_total, lon_t...  62.3 us
    unnamed x2, local copies, waits for them, and re-layouts  2.14 us

profile of v2, /device:TPU:1, one launch (start us, length us, event | category | flops | bytes accessed | tf_op | source)
XLA Modules:
  0.0 65.7 jit_solution(13232939718590126614)
XLA Ops:
  1.3 62.3 %solve.1 = (bf16[64,128,128]{2,1,0:T(8,128)(2,1)S(1)}, f32[1152,128]{1,0:T(8,128)S(1)}) custom-call(s32[1]{0:T(128)S(6)} %copy.12.live_ref, bf16[1024,128]{1,0:T(8,128)(2,1)} %rows_hbm.1, s32[1,1024]{1,0:T(1,128)} %bitcast.6, s32[1,1024]{1,0:T(1,128)} %bitcast.7, s32[1,1024]{1,0:T(1,128)} %bitcast.8, bf16[2,1024]{1,0:T(2,128)(2,1)} %bitcast.9, ...), custom_call_target="tpu_custom_call" | custom-call | tf_op jit(solution)/shard_map/solve/pallas_call | solution.py:540
  63.6 1.3 %copy.13 = bf16[64,128,128]{2,1,0:T(8,128)(2,1)} copy(bf16[64,128,128]{2,1,0:T(8,128)(2,1)S(1)} %get-tuple-element.8) | data formatting | bytes 4194304
  64.9 0.8 %copy.14 = f32[3,3,128,128]{3,2,1,0:T(8,128)} copy(f32[3,3,128,128]{3,2,1,0:T(8,128)S(1)} %bitcast.5) | data formatting | bytes 1179648

commit v3 on v2

--- a/solution.py
+++ b/solution.py
@@ -33,15 +33,19 @@
     wg_ref,
     *refs,
 ):
-    (rows_ref, owner_ref, lat_ref, lon_ref, pos_ref, feat_ref, weight_ref) = refs[:7]
-    (held, inbox, sums, canvas, lat_taps, lon_taps, halves) = refs[7:14]
-    strips, landed = refs[14:22], refs[22:30]
-    (windows, turned, total, flat, mixer, pieces, twin, parts, mine, gathered) = refs[30:40]
-    (load_sem, send_sem, recv_sem) = refs[40:43]
-    halo_send, halo_recv, pair_send, pair_recv, part_send, part_recv, all_send, all_recv = refs[43:]
+    (rows_ref, owner_ref, lat_ref, lon_ref, pos_ref, weight_ref) = refs[:6]
+    (field, beside_left, beside_right, beside, edges) = refs[6:11]
+    (held, inbox, sums, canvas, lat_taps, lon_taps, halves) = refs[11:18]
+    strips, landed = refs[18:26], refs[26:34]
+    (windows, turned, total, flat, mixer, pieces, twin, parts, mine, gathered) = refs[34:44]
+    (load_sem, send_sem, recv_sem, field_send, field_recv) = refs[44:49]
+    halo_send, halo_recv, pair_send, pair_recv, part_send, part_recv, all_send, all_recv = refs[49:]
     devices = inbox.shape[0]
     row_total, channels = rows_ref.shape
-    tile_lat, tile_lon = feat_ref.shape[:2]
+    tile_lat, tile_lon = ig_ref.shape[:2]
+    up, down = before + 1, after + 1
+    tall = canvas.shape[0]
+    own_field = field.at[up : up + tile_lat]
     lat, lon = lax.axis_index("lat"), lax.axis_index("lon")
     me = lon * lat_total + lat
     span = halves.shape[0]
@@ -67,7 +71,7 @@
         for k, (src, dst) in enumerate(
             zip(
                 (rows_hbm, owner_hbm, lat_hbm, lon_hbm, pos_hbm, feat_hbm, weight_hbm),
-                (rows_ref, owner_ref, lat_ref, lon_ref, pos_ref, feat_ref, weight_ref),
+                (rows_ref, owner_ref, lat_ref, lon_ref, pos_ref, own_field, weight_ref),
             )
         )
     ]
@@ -78,8 +82,20 @@
     mixer[...] = jnp.zeros_like(mixer)
     total[...] = jnp.zeros_like(total)
     rows, cols = tile_lat + 2, tile_lon + 2
-    turned[:, 0 : 2 * tile_lon] = jnp.zeros((channels, 2 * tile_lon), bf16)
-    turned[:, rows * tile_lon : (rows + 2) * tile_lon] = jnp.zeros((channels, 2 * tile_lon), bf16)
+    field[tall + 1] = jnp.zeros(field.shape[1:], bf16)
+    for ref in (beside_left, beside_right):
+        ref[tall + 1] = jnp.zeros(ref.shape[1:], bf16)
+
+    @pl.when(lat == 0)
+    def _():
+        for ref in (field, beside_left, beside_right):
+            ref[0:up] = jnp.zeros((up,) + ref.shape[1:], bf16)
+
+    @pl.when(lat == lat_total - 1)
+    def _():
+        for ref in (field, beside_left, beside_right):
+            ref[up + tile_lat : tall + 1] = jnp.zeros((down,) + ref.shape[1:], bf16)
+
     for load in loads[:5]:
         load.wait()
 
@@ -173,11 +189,48 @@
 
     loads[5].wait()
 
-    def turn(p, _):
-        turned[:, pl.ds(pl.multiple_of((p + 2) * tile_lon, tile_lon), tile_lon)] = feat_ref[p].T
-        return 0
-
-    lax.fori_loop(0, tile_lat, turn, 0)
+    def when(da, cond, fn):
+        if da == 0:
+            fn()
+        else:
+            pl.when(cond)(fn)
+
+    ways = ((-1, 0), (1, 0), (0, -1), (0, 1), (-1, -1), (-1, 1), (1, -1), (1, 1))
+    reach = beside_left.shape[1]
+    source_rows = {-1: slice(up, up + down), 0: slice(up, up + tile_lat), 1: slice(tile_lat, up + tile_lat)}
+    target_rows = {-1: slice(up + tile_lat, tall + 1), 0: source_rows[0], 1: slice(0, up)}
+    source_cols = {-1: slice(0, reach), 0: slice(0, tile_lon), 1: slice(tile_lon - reach, tile_lon)}
+    target_of = {-1: beside_right, 0: field, 1: beside_left}
+    borders = []
+    for w, (da, db) in enumerate(ways):
+        copy = pltpu.make_async_remote_copy(
+            src_ref=field.at[source_rows[da], source_cols[db]],
+            dst_ref=target_of[db].at[target_rows[da]],
+            send_sem=field_send.at[w],
+            recv_sem=field_recv.at[w],
+            device_id=((lat + da + lat_total) % lat_total, (lon + db + lon_total) % lon_total),
+            device_id_type=pl.DeviceIdType.MESH,
+        )
+        sends = (lat + da >= 0) & (lat + da < lat_total)
+        takes = (lat - da >= 0) & (lat - da < lat_total)
+        borders.append((copy, sends, takes))
+    for (copy, sends, _), (da, _) in zip(borders, ways):
+        when(da, sends, copy.start)
+
+    def turn(p):
+        at = p * tile_lon
+        if not isinstance(p, int):
+            at = pl.multiple_of(at, tile_lon)
+        turned[:, pl.ds(at, tile_lon)] = field[p].T
+
+    fast = math.gcd(tile_lat, 8)
+
+    def turn_some(k, _):
+        for j in range(fast):
+            turn(up + k * fast + j)
+        return 0
+
+    lax.fori_loop(0, tile_lat // fast, turn_some, 0)
     loads[6].wait()
     for a in range(3):
         for b in range(3):
@@ -190,8 +243,8 @@
     line_lon = lax.broadcasted_iota(jnp.int32, (lon_taps.shape[0], span), 0).astype(f32)
     lanes = lax.broadcasted_iota(jnp.int32, (8, 128), 1) // capacity
     wide = sums.shape[1]
-    deep = lon_taps.shape[0]
-    stride = 8
+    line_lon = jnp.where(line_lon >= wide, line_lon - wide, line_lon)
+    stride = next(n for n in (24, 12, 8, 4, 2) if tall % n == 0)
 
     def taps_of(line, base, frac):
         tap = line - base
@@ -234,34 +287,57 @@
 
         def add(k, _):
             lhs = []
-            for j in range(stride):
-                row = jnp.broadcast_to(lat_taps[pl.ds(k * stride + j, 1), :], (16, span)).astype(bf16)
-                for t in range(deep // 16):
-                    lhs.append(row * lon_taps[t * 16 : (t + 1) * 16, :])
+            for j in range(0, stride, 2):
+                pair = [
+                    jnp.broadcast_to(lat_taps[pl.ds(k * stride + j + n, 1), :], (8, span))
+                    for n in range(2)
+                ]
+                for t in range(0, 2 * wide, 16):
+                    row = jnp.concatenate([pair[t // wide], pair[(t + 8) // wide]], axis=0)
+                    lhs.append(row.astype(bf16) * lon_taps[t : t + 16, :])
             out = jnp.dot(jnp.concatenate(lhs, axis=0), halves[...], preferred_element_type=f32)
             for j in range(stride):
-                sums[k * stride + j] += out[j * deep : j * deep + wide]
+                sums[k * stride + j] += out[j * wide : (j + 1) * wide]
             return 0
 
-        lax.fori_loop(0, sums.shape[0] // stride, add, 0)
-
-    for q in order[::-1]:
+        lax.fori_loop(0, tall // stride, add, 0)
+
+    def border():
+        for (copy, _, takes), (da, _) in zip(borders, ways):
+            when(da, takes, copy.wait_recv)
+        for p in (*range(up), *range(up + tile_lat, tall + 2)):
+            turn(p)
+        slots = 2 * reach
+        some = 128 // slots
+        for a in range(3):
+            for k in range(tall // some):
+                at = slice(a + k * some, a + (k + 1) * some)
+                both = jnp.concatenate([beside_left[at], beside_right[at]], axis=1)
+                beside[a * channels : (a + 1) * channels, k * 128 : (k + 1) * 128] = both.reshape(
+                    128, channels
+                ).T
+
+    for k, q in enumerate(order[::-1]):
+        if k == groups - 1:
+            border()
         collect(q)
 
-    tall = canvas.shape[0]
+    pad = reach
 
     def join(i, _):
-        canvas[i, 0:half, :] = sums[i, 0:half, 0:channels]
-        canvas[i, half:wide, :] = (
+        canvas[i, 0:pad, :] = jnp.zeros((pad, channels), f32)
+        canvas[i, pad : pad + half, :] = sums[i, 0:half, 0:channels]
+        canvas[i, pad + half : pad + wide, :] = (
             sums[i, half:wide, 0:channels] + sums[i, 0 : wide - half, channels : 2 * channels]
         )
-        canvas[i, wide : wide + half, :] = sums[i, wide - half : wide, channels : 2 * channels]
+        canvas[i, pad + wide : pad + wide + half, :] = sums[i, wide - half : wide, channels : 2 * channels]
+        canvas[i, pad + wide + half : 2 * pad + wide + half, :] = jnp.zeros((pad, channels), f32)
         return 0
 
     lax.fori_loop(0, tall, join, 0)
-    up, down = before + 1, after + 1
     inset = before - 1
-    spans = ((0, up), (inset, cols), (inset + cols - 2, down))
+    edge = pad + inset
+    spans = ((pad, up), (edge, cols), (edge + cols - 2, down))
     for count, first, refs in (
         (up, 0, (strips[4], strips[0], strips[5])),
         (down, inset + rows - 2, (strips[6], strips[1], strips[7])),
@@ -271,13 +347,12 @@
                 ref[i] = canvas[first + i, start : start + width, :].astype(bf16)
 
     def emit(i, _):
-        strips[2][i] = canvas[i + inset, 0:up, :].astype(bf16)
-        strips[3][i] = canvas[i + inset, inset + cols - 2 : inset + cols - 2 + down, :].astype(bf16)
+        strips[2][i] = canvas[i + inset, pad : pad + up, :].astype(bf16)
+        strips[3][i] = canvas[i + inset, edge + cols - 2 : edge + cols - 2 + down, :].astype(bf16)
         return 0
 
     lax.fori_loop(0, rows, emit, 0)
 
-    ways = ((-1, 0), (1, 0), (0, -1), (0, 1), (-1, -1), (-1, 1), (1, -1), (1, 1))
     chips = devices // 2
     at = lat * lon_total + lon
     core, chip = at % 2, at // 2
@@ -300,50 +375,38 @@
         takes = (lat - da >= 0) & (lat - da < lat_total)
         halos.append((copy, sends, takes))
 
-    def when(da, cond, fn):
-        if da == 0:
-            fn()
-        else:
-            pl.when(cond)(fn)
-
     for (copy, sends, _), (da, _) in zip(halos, ways):
         when(da, sends, copy.start)
 
-    for (copy, _, takes), (da, db), ref in zip(halos, ways, landed):
-
-        def take(copy=copy, da=da, db=db, ref=ref):
-            copy.wait_recv()
-            high = {-1: rows - up, 0: 0, 1: 0}[da]
-            count = {-1: up, 0: rows, 1: down}[da]
-            left = {-1: cols - up, 0: 0, 1: 0}[db]
-            width = {-1: up, 0: cols, 1: down}[db]
-
-            def add(i, _):
-                canvas[inset + high + i, inset + left : inset + left + width, :] += ref[i].astype(f32)
-                return 0
-
-            lax.fori_loop(0, count, add, 0)
-
-        when(da, takes, take)
-
     @pl.when(lat == 0)
     def _():
-        canvas[inset] = jnp.zeros(canvas.shape[1:], f32)
+        canvas[0:before] = jnp.zeros((before,) + canvas.shape[1:], f32)
 
     @pl.when(lat == lat_total - 1)
     def _():
-        canvas[inset + rows - 1] = jnp.zeros(canvas.shape[1:], f32)
+        canvas[before + tile_lat : tall] = jnp.zeros((tall - before - tile_lat,) + canvas.shape[1:], f32)
 
     def shift(i, _):
         at = pl.ds(pl.multiple_of(i * tile_lon, tile_lon), tile_lon)
         for b in range(3):
             windows[at, b * channels : (b + 1) * channels] = canvas[
-                i + inset, inset + 2 - b : inset + 2 - b + tile_lon, :
+                i, edge + 2 - b : edge + 2 - b + tile_lon, :
             ].astype(bf16)
         return 0
 
-    lax.fori_loop(0, rows, shift, 0)
-    step = next(n for n in (11, 6, 3, 2, 1) if rows % n == 0)
+    lax.fori_loop(0, tall, shift, 0)
+
+    def shift_edges(i, _):
+        at = pl.ds(pl.multiple_of(i * 2 * reach, 2 * reach), 2 * reach)
+        for b in range(3):
+            first = edge + 2 - b - reach
+            second = edge + 2 - b + tile_lon
+            both = [canvas[i, first : first + reach, :], canvas[i, second : second + reach, :]]
+            edges[at, b * channels : (b + 1) * channels] = jnp.concatenate(both, axis=0).astype(bf16)
+        return 0
+
+    lax.fori_loop(0, tall, shift_edges, 0)
+    step = next(n for n in (12, 8, 6, 4, 3, 2, 1) if tall % n == 0)
     depth = step * tile_lon
 
     def weigh(k, _):
@@ -359,7 +422,8 @@
         total[...] += jnp.dot(lhs, rhs, preferred_element_type=f32)
         return 0
 
-    lax.fori_loop(0, rows // step, weigh, 0)
+    lax.fori_loop(0, tall // step, weigh, 0)
+    total[...] += jnp.dot(beside[...], edges[...], preferred_element_type=f32)
     for a in range(3):
         for b in range(3):
             at = (a * 3 + b) * channels
@@ -375,7 +439,7 @@
     lax.fori_loop(0, devices, cut, 0)
     part = math.gcd(tile_lat // 2, 8)
     strides = tile_lat // 2 // part
-    first, second = strides // 4, strides * 3 // 4
+    first = strides // 2
 
     def apply(k, _):
         lhs = jnp.concatenate(
@@ -384,7 +448,9 @@
                     [
                         windows[
                             pl.ds(
-                                pl.multiple_of((2 * (k * part + j) + r) * tile_lon, tile_lon),
+                                pl.multiple_of(
+                                    (inset + 2 * (k * part + j) + r) * tile_lon, tile_lon
+                                ),
                                 tile_lon,
                             ),
                             :,
@@ -405,6 +471,33 @@
                 ]
         return 0
 
+    def settle():
+        for (copy, _, takes), (da, db), ref in zip(halos, ways, landed):
+
+            def take(copy=copy, da=da, db=db, ref=ref):
+                copy.wait_recv()
+                high = {-1: rows - up, 0: 0, 1: 0}[da]
+                count = {-1: up, 0: rows, 1: down}[da]
+                left = {-1: cols - up, 0: 0, 1: 0}[db]
+                width = {-1: up, 0: cols, 1: down}[db]
+
+                def add(i, _):
+                    canvas[inset + high + i, edge + left : edge + left + width, :] += ref[i].astype(f32)
+                    return 0
+
+                lax.fori_loop(0, count, add, 0)
+
+            when(da, takes, take)
+
+        @pl.when(lat == 0)
+        def _():
+            canvas[inset] = jnp.zeros(canvas.shape[1:], f32)
+
+        @pl.when(lat == lat_total - 1)
+        def _():
+            canvas[inset + rows - 1] = jnp.zeros(canvas.shape[1:], f32)
+        lax.fori_loop(inset, inset + rows, shift, 0)
+
     def paired(src, dst, n):
         return pltpu.make_async_remote_copy(
             src_ref=src,
@@ -444,7 +537,6 @@
 
     swap = paired(pieces.at[pl.ds(other * chips, chips)], twin, 0)
     swap.start()
-    lax.fori_loop(0, first, apply, 0)
     swap.wait_recv()
 
     def merge(p, _):
@@ -454,7 +546,8 @@
 
     lax.fori_loop(0, chips, merge, 0)
     each_chip(lambda peer: scattered(peer, chip).start())
-    lax.fori_loop(first, second, apply, 0)
+    settle()
+    lax.fori_loop(0, first, apply, 0)
     parts[chip] = pieces[core * chips + chip]
     each_chip(lambda peer: scattered(peer, peer).wait_recv())
 
@@ -466,7 +559,7 @@
     ).astype(bf16)
     each_chip(lambda peer: shared(peer, chip).start())
     gathered[core * chips + chip] = mine[...]
-    lax.fori_loop(second, strides, apply, 0)
+    lax.fori_loop(first, strides, apply, 0)
     each_chip(lambda peer: shared(peer, peer).wait_recv())
     kept = gathered.at[pl.ds(core * chips, chips)]
     back = paired(kept, kept, 1)
@@ -479,7 +572,7 @@
     lax.fori_loop(core * chips, (core + 1) * chips, spill, 0)
     back.wait_recv()
     lax.fori_loop(other * chips, (other + 1) * chips, spill, 0)
-    for (copy, sends, _), (da, _) in zip(halos, ways):
+    for (copy, sends, _), (da, _) in zip(halos + borders, ways + ways):
         when(da, sends, copy.wait_send)
     swap.wait_send()
     back.wait_send()
@@ -545,21 +638,26 @@
         ],
         in_specs=[smem] + [pl.BlockSpec(memory_space=pltpu.HBM)] * 7,
         out_specs=[vmem] * 2,
-        scratch_shapes=[pltpu.VMEM(x.shape, x.dtype) for x in operands]
+        scratch_shapes=[pltpu.VMEM(x.shape, x.dtype) for x in operands if x is not features]
         + [
+            pltpu.VMEM((tall + 2, tile_lon, channels), bf16),
+            pltpu.VMEM((tall + 2, 8, channels), bf16),
+            pltpu.VMEM((tall + 2, 8, channels), bf16),
+            pltpu.VMEM((3 * channels, tall * 16), bf16),
+            pltpu.VMEM((tall * 16, 3 * channels), bf16),
             pltpu.VMEM(message, bf16),
             pltpu.VMEM(message, bf16),
             pltpu.VMEM((tall, wide, 2 * channels), f32),
-            pltpu.VMEM((tall, wide + tile_lon // 2, channels), f32),
+            pltpu.VMEM((tall, wide + tile_lon // 2 + 16, channels), f32),
             pltpu.VMEM((tall, span), f32),
-            pltpu.VMEM((-(-wide // 16) * 16, span), bf16),
+            pltpu.VMEM((2 * wide, span), bf16),
             pltpu.VMEM((span, 2 * channels), bf16),
         ]
         + places
         + places
         + [
-            pltpu.VMEM((rows * tile_lon, 3 * channels), bf16),
-            pltpu.VMEM((channels, (rows + 2) * tile_lon), bf16),
+            pltpu.VMEM((tall * tile_lon, 3 * channels), bf16),
+            pltpu.VMEM((channels, (tall + 2) * tile_lon), bf16),
             pltpu.VMEM((3 * channels, 3 * channels), f32),
             pltpu.VMEM((flat_rows, channels), f32),
             pltpu.VMEM((4 * 3 * channels, 2 * channels), bf16),
@@ -571,6 +669,8 @@
             dma((7,)),
             dma((device_total,)),
             dma((device_total,)),
+            dma((8,)),
+            dma((8,)),
             dma((8,)),
             dma((8,)),
             dma((2,)),

time: 65.9 us -> 56.8 us (0.86)
  Pallas kernels: 62.3 us -> 53.2 us
    pallas_call x1, Pallas kernels: 62.3 us -> 53.2 us  [shards(): pl.pallas_call(functools.partial(solve_kernel, capacity, lat_total, lon_t...]
where the time goes in v3:
time: 56.8 us; the launch traced here: 56.6 us
  Pallas kernels  53.2 us (94%)
  local copies, waits for them, and re-layouts  2.14 us (4%)
  between operations  1.29 us (2%)
    pallas_call x1, Pallas kernels, shards(): pl.pallas_call(functools.partial(solve_kernel, capacity, lat_total, lon_t...  53.2 us
    unnamed x2, local copies, waits for them, and re-layouts  2.14 us

profile of v3, /device:TPU:1, one launch (start us, length us, event | category | flops | bytes accessed | tf_op | source)
XLA Modules:
  0.0 56.6 jit_solution(14242891721954082398)
XLA Ops:
  1.3 53.2 %solve.1 = (bf16[64,128,128]{2,1,0:T(8,128)(2,1)S(1)}, f32[1152,128]{1,0:T(8,128)S(1)}) custom-call(s32[1]{0:T(128)S(6)} %copy.12.live_ref, bf16[1024,128]{1,0:T(8,128)(2,1)} %rows_hbm.1, s32[1,1024]{1,0:T(1,128)} %bitcast.6, s32[1,1024]{1,0:T(1,128)} %bitcast.7, s32[1,1024]{1,0:T(1,128)} %bitcast.8, bf16[2,1024]{1,0:T(2,128)(2,1)} %bitcast.9, ...), custom_call_target="tpu_custom_call" | custom-call | tf_op jit(solution)/shard_map/solve/pallas_call | solution.py:633
  54.5 1.3 %copy.13 = bf16[64,128,128]{2,1,0:T(8,128)(2,1)} copy(bf16[64,128,128]{2,1,0:T(8,128)(2,1)S(1)} %get-tuple-element.8) | data formatting | bytes 4194304
  55.8 0.8 %copy.14 = f32[3,3,128,128]{3,2,1,0:T(8,128)} copy(f32[3,3,128,128]{3,2,1,0:T(8,128)S(1)} %bitcast.5) | data formatting | bytes 1179648

commit v4 on v3

--- a/solution.py
+++ b/solution.py
@@ -34,12 +34,12 @@
     *refs,
 ):
     (rows_ref, owner_ref, lat_ref, lon_ref, pos_ref, weight_ref) = refs[:6]
-    (field, beside_left, beside_right, beside, edges) = refs[6:11]
-    (held, inbox, sums, canvas, lat_taps, lon_taps, halves) = refs[11:18]
-    strips, landed = refs[18:26], refs[26:34]
-    (windows, turned, total, flat, mixer, pieces, twin, parts, mine, gathered) = refs[34:44]
-    (load_sem, send_sem, recv_sem, field_send, field_recv) = refs[44:49]
-    halo_send, halo_recv, pair_send, pair_recv, part_send, part_recv, all_send, all_recv = refs[49:]
+    (field, stage, beside, edges) = refs[6:10]
+    (held, inbox, sums, canvas, lat_taps, lon_taps, halves) = refs[10:17]
+    strips, landed = refs[17:25], refs[25:33]
+    (windows, turned, total, flat, mixer, pieces, twin, parts, mine, gathered) = refs[33:43]
+    (load_sem, send_sem, recv_sem, field_send, field_recv) = refs[43:48]
+    halo_send, halo_recv, pair_send, pair_recv, part_send, part_recv, all_send, all_recv = refs[48:]
     devices = inbox.shape[0]
     row_total, channels = rows_ref.shape
     tile_lat, tile_lon = ig_ref.shape[:2]
@@ -82,19 +82,16 @@
     mixer[...] = jnp.zeros_like(mixer)
     total[...] = jnp.zeros_like(total)
     rows, cols = tile_lat + 2, tile_lon + 2
+    stage[...] = jnp.zeros_like(stage)
     field[tall + 1] = jnp.zeros(field.shape[1:], bf16)
-    for ref in (beside_left, beside_right):
-        ref[tall + 1] = jnp.zeros(ref.shape[1:], bf16)
 
     @pl.when(lat == 0)
     def _():
-        for ref in (field, beside_left, beside_right):
-            ref[0:up] = jnp.zeros((up,) + ref.shape[1:], bf16)
+        field[0:up] = jnp.zeros((up,) + field.shape[1:], bf16)
 
     @pl.when(lat == lat_total - 1)
     def _():
-        for ref in (field, beside_left, beside_right):
-            ref[up + tile_lat : tall + 1] = jnp.zeros((down,) + ref.shape[1:], bf16)
+        field[up + tile_lat : tall + 1] = jnp.zeros((down,) + field.shape[1:], bf16)
 
     for load in loads[:5]:
         load.wait()
@@ -179,10 +176,13 @@
     per = group // chunk
     steps = [(q, c) for q in order for c in range(per)]
     first_of = [q * group + c * chunk for q, c in steps]
-    build(first_of[0])
+    early = len(first_of) // 2
+    for first in first_of[:early]:
+        build(first)
     pl.semaphore_wait(barrier, devices - 1)
-    send(first_of[0])
-    for first in first_of[1:]:
+    for first in first_of[:early]:
+        send(first)
+    for first in first_of[early:]:
         build(first)
         send(first)
     inbox[me] = held[me]
@@ -196,19 +196,20 @@
             pl.when(cond)(fn)
 
     ways = ((-1, 0), (1, 0), (0, -1), (0, 1), (-1, -1), (-1, 1), (1, -1), (1, 1))
-    reach = beside_left.shape[1]
-    source_rows = {-1: slice(up, up + down), 0: slice(up, up + tile_lat), 1: slice(tile_lat, up + tile_lat)}
-    target_rows = {-1: slice(up + tile_lat, tall + 1), 0: source_rows[0], 1: slice(0, up)}
-    source_cols = {-1: slice(0, reach), 0: slice(0, tile_lon), 1: slice(tile_lon - reach, tile_lon)}
-    target_of = {-1: beside_right, 0: field, 1: beside_left}
+    reach = 8
     borders = []
-    for w, (da, db) in enumerate(ways):
+    for w, (da, source, target) in enumerate(
+        (
+            (-1, slice(up, up + down), slice(up + tile_lat, tall + 1)),
+            (1, slice(tile_lat, up + tile_lat), slice(0, up)),
+        )
+    ):
         copy = pltpu.make_async_remote_copy(
-            src_ref=field.at[source_rows[da], source_cols[db]],
-            dst_ref=target_of[db].at[target_rows[da]],
+            src_ref=field.at[source],
+            dst_ref=field.at[target],
             send_sem=field_send.at[w],
             recv_sem=field_recv.at[w],
-            device_id=((lat + da + lat_total) % lat_total, (lon + db + lon_total) % lon_total),
+            device_id=((lat + da + lat_total) % lat_total, lon),
             device_id_type=pl.DeviceIdType.MESH,
         )
         sends = (lat + da >= 0) & (lat + da < lat_total)
@@ -312,12 +313,14 @@
         for a in range(3):
             for k in range(tall // some):
                 at = slice(a + k * some, a + (k + 1) * some)
-                both = jnp.concatenate([beside_left[at], beside_right[at]], axis=1)
+                both = jnp.concatenate(
+                    [field[at, 0:reach], field[at, tile_lon - reach : tile_lon]], axis=1
+                )
                 beside[a * channels : (a + 1) * channels, k * 128 : (k + 1) * 128] = both.reshape(
                     128, channels
                 ).T
 
-    for k, q in enumerate(order[::-1]):
+    for k, q in enumerate([order[3], order[2], order[0], order[1]] if groups == 4 else order[::-1]):
         if k == groups - 1:
             border()
         collect(q)
@@ -337,30 +340,25 @@
     lax.fori_loop(0, tall, join, 0)
     inset = before - 1
     edge = pad + inset
-    spans = ((pad, up), (edge, cols), (edge + cols - 2, down))
-    for count, first, refs in (
-        (up, 0, (strips[4], strips[0], strips[5])),
-        (down, inset + rows - 2, (strips[6], strips[1], strips[7])),
-    ):
-        for i in range(count):
-            for (start, width), ref in zip(spans, refs):
-                ref[i] = canvas[first + i, start : start + width, :].astype(bf16)
-
-    def emit(i, _):
-        strips[2][i] = canvas[i + inset, pad : pad + up, :].astype(bf16)
-        strips[3][i] = canvas[i + inset, edge + cols - 2 : edge + cols - 2 + down, :].astype(bf16)
-        return 0
-
-    lax.fori_loop(0, rows, emit, 0)
-
-    chips = devices // 2
-    at = lat * lon_total + lon
-    core, chip = at % 2, at // 2
-    other = 1 - core
-
-    def seat(peer):
-        return (peer // lon_total, peer % lon_total)
-
+
+    @pl.when(lat == 0)
+    def _():
+        canvas[0:before] = jnp.zeros((before,) + canvas.shape[1:], f32)
+
+    @pl.when(lat == lat_total - 1)
+    def _():
+        canvas[before + tile_lat : tall] = jnp.zeros((tall - before - tile_lat,) + canvas.shape[1:], f32)
+
+    some = math.gcd(tall, 4)
+
+    def emit(k, _):
+        for j in range(some):
+            i = k * some + j
+            strips[2][i] = canvas[i, pad : pad + up, :].astype(bf16)
+            strips[3][i] = canvas[i, edge + cols - 2 : edge + cols - 2 + down, :].astype(bf16)
+        return 0
+
+    lax.fori_loop(0, tall // some, emit, 0)
     halos = []
     for w, (da, db) in enumerate(ways):
         copy = pltpu.make_async_remote_copy(
@@ -374,17 +372,27 @@
         sends = (lat + da >= 0) & (lat + da < lat_total)
         takes = (lat - da >= 0) & (lat - da < lat_total)
         halos.append((copy, sends, takes))
-
+    beside_halos = halos[2:4]
+    for copy, _, _ in beside_halos:
+        copy.start()
+    spans = ((pad, up), (edge, cols), (edge + cols - 2, down))
+    for count, first, refs in (
+        (up, 0, (strips[4], strips[0], strips[5])),
+        (down, inset + rows - 2, (strips[6], strips[1], strips[7])),
+    ):
+        for i in range(count):
+            for (start, width), ref in zip(spans, refs):
+                ref[i] = canvas[first + i, start : start + width, :].astype(bf16)
     for (copy, sends, _), (da, _) in zip(halos, ways):
-        when(da, sends, copy.start)
-
-    @pl.when(lat == 0)
-    def _():
-        canvas[0:before] = jnp.zeros((before,) + canvas.shape[1:], f32)
-
-    @pl.when(lat == lat_total - 1)
-    def _():
-        canvas[before + tile_lat : tall] = jnp.zeros((tall - before - tile_lat,) + canvas.shape[1:], f32)
+        if da != 0:
+            pl.when(sends)(copy.start)
+    chips = devices // 2
+    at = lat * lon_total + lon
+    core, chip = at % 2, at // 2
+    other = 1 - core
+
+    def seat(peer):
+        return (peer // lon_total, peer % lon_total)
 
     def shift(i, _):
         at = pl.ds(pl.multiple_of(i * tile_lon, tile_lon), tile_lon)
@@ -396,16 +404,20 @@
 
     lax.fori_loop(0, tall, shift, 0)
 
-    def shift_edges(i, _):
-        at = pl.ds(pl.multiple_of(i * 2 * reach, 2 * reach), 2 * reach)
-        for b in range(3):
-            first = edge + 2 - b - reach
-            second = edge + 2 - b + tile_lon
-            both = [canvas[i, first : first + reach, :], canvas[i, second : second + reach, :]]
-            edges[at, b * channels : (b + 1) * channels] = jnp.concatenate(both, axis=0).astype(bf16)
-        return 0
-
-    lax.fori_loop(0, tall, shift_edges, 0)
+    def shift_edges(k, _):
+        for j in range(some):
+            i = k * some + j
+            stage[i, 0:down] = landed[3][i].astype(f32)
+            stage[i, 3 * reach : 3 * reach + up] = landed[2][i].astype(f32)
+            at = pl.ds(pl.multiple_of(i * 2 * reach, 2 * reach), 2 * reach)
+            for b in range(3):
+                first, second = 2 - b, 2 * reach + up - b
+                both = [stage[i, first : first + reach, :], stage[i, second : second + reach, :]]
+                edges[at, b * channels : (b + 1) * channels] = jnp.concatenate(
+                    both, axis=0
+                ).astype(bf16)
+        return 0
+
     step = next(n for n in (12, 8, 6, 4, 3, 2, 1) if tall % n == 0)
     depth = step * tile_lon
 
@@ -423,6 +435,9 @@
         return 0
 
     lax.fori_loop(0, tall // step, weigh, 0)
+    for copy, _, _ in beside_halos:
+        copy.wait_recv()
+    lax.fori_loop(0, tall // some, shift_edges, 0)
     total[...] += jnp.dot(beside[...], edges[...], preferred_element_type=f32)
     for a in range(3):
         for b in range(3):
@@ -475,27 +490,21 @@
         for (copy, _, takes), (da, db), ref in zip(halos, ways, landed):
 
             def take(copy=copy, da=da, db=db, ref=ref):
-                copy.wait_recv()
-                high = {-1: rows - up, 0: 0, 1: 0}[da]
-                count = {-1: up, 0: rows, 1: down}[da]
+                if da != 0:
+                    copy.wait_recv()
+                high = {-1: inset + rows - up, 0: 0, 1: inset}[da]
+                count = {-1: up, 0: tall, 1: down}[da]
                 left = {-1: cols - up, 0: 0, 1: 0}[db]
                 width = {-1: up, 0: cols, 1: down}[db]
 
                 def add(i, _):
-                    canvas[inset + high + i, edge + left : edge + left + width, :] += ref[i].astype(f32)
+                    canvas[high + i, edge + left : edge + left + width, :] += ref[i].astype(f32)
                     return 0
 
                 lax.fori_loop(0, count, add, 0)
 
             when(da, takes, take)
 
-        @pl.when(lat == 0)
-        def _():
-            canvas[inset] = jnp.zeros(canvas.shape[1:], f32)
-
-        @pl.when(lat == lat_total - 1)
-        def _():
-            canvas[inset + rows - 1] = jnp.zeros(canvas.shape[1:], f32)
         lax.fori_loop(inset, inset + rows, shift, 0)
 
     def paired(src, dst, n):
@@ -572,7 +581,7 @@
     lax.fori_loop(core * chips, (core + 1) * chips, spill, 0)
     back.wait_recv()
     lax.fori_loop(other * chips, (other + 1) * chips, spill, 0)
-    for (copy, sends, _), (da, _) in zip(halos + borders, ways + ways):
+    for (copy, sends, _), (da, _) in zip(halos + borders, ways + ways[:2]):
         when(da, sends, copy.wait_send)
     swap.wait_send()
     back.wait_send()
@@ -607,8 +616,8 @@
     strip_shapes = [
         (up, cols),
         (down, cols),
-        (rows, up),
-        (rows, down),
+        (tall, up),
+        (tall, down),
         (up, up),
         (up, down),
         (down, up),
@@ -641,8 +650,7 @@
         scratch_shapes=[pltpu.VMEM(x.shape, x.dtype) for x in operands if x is not features]
         + [
             pltpu.VMEM((tall + 2, tile_lon, channels), bf16),
-            pltpu.VMEM((tall + 2, 8, channels), bf16),
-            pltpu.VMEM((tall + 2, 8, channels), bf16),
+            pltpu.VMEM((tall, 32, channels), f32),
             pltpu.VMEM((3 * channels, tall * 16), bf16),
             pltpu.VMEM((tall * 16, 3 * channels), bf16),
             pltpu.VMEM(message, bf16),
@@ -669,8 +677,8 @@
             dma((7,)),
             dma((device_total,)),
             dma((device_total,)),
-            dma((8,)),
-            dma((8,)),
+            dma((2,)),
+            dma((2,)),
             dma((8,)),
             dma((8,)),
             dma((2,)),

time: 56.8 us -> 54.1 us (0.952)
  Pallas kernels: 53.2 us -> 50.5 us
    pallas_call x1, Pallas kernels: 53.2 us -> 50.5 us  [shards(): pl.pallas_call(functools.partial(solve_kernel, capacity, lat_total, lon_t...]
where the time goes in v4:
time: 54.1 us; the launch traced here: 53.9 us
  Pallas kernels  50.5 us (93%)
  local copies, waits for them, and re-layouts  2.14 us (4%)
  between operations  1.29 us (2%)
    pallas_call x1, Pallas kernels, shards(): pl.pallas_call(functools.partial(solve_kernel, capacity, lat_total, lon_t...  50.5 us
    unnamed x2, local copies, waits for them, and re-layouts  2.14 us

profile of v4, /device:TPU:1, one launch (start us, length us, event | category | flops | bytes accessed | tf_op | source)
XLA Modules:
  0.0 53.9 jit_solution(9744263103529199431)
XLA Ops:
  1.3 50.5 %solve.1 = (bf16[64,128,128]{2,1,0:T(8,128)(2,1)S(1)}, f32[1152,128]{1,0:T(8,128)S(1)}) custom-call(s32[1]{0:T(128)S(6)} %copy.12.live_ref, bf16[1024,128]{1,0:T(8,128)(2,1)} %rows_hbm.1, s32[1,1024]{1,0:T(1,128)} %bitcast.6, s32[1,1024]{1,0:T(1,128)} %bitcast.7, s32[1,1024]{1,0:T(1,128)} %bitcast.8, bf16[2,1024]{1,0:T(2,128)(2,1)} %bitcast.9, ...), custom_call_target="tpu_custom_call" | custom-call | tf_op jit(solution)/shard_map/solve/pallas_call | solution.py:642
  51.8 1.3 %copy.13 = bf16[64,128,128]{2,1,0:T(8,128)(2,1)} copy(bf16[64,128,128]{2,1,0:T(8,128)(2,1)S(1)} %get-tuple-element.8) | data formatting | bytes 4194304
  53.1 0.8 %copy.14 = f32[3,3,128,128]{3,2,1,0:T(8,128)} copy(f32[3,3,128,128]{3,2,1,0:T(8,128)S(1)} %bitcast.5) | data formatting | bytes 1179648

commit v5 on v4

--- a/solution.py
+++ b/solution.py
@@ -30,16 +30,16 @@
     feat_hbm,
     weight_hbm,
     ig_ref,
-    wg_ref,
+    gathered,
     *refs,
 ):
     (rows_ref, owner_ref, lat_ref, lon_ref, pos_ref, weight_ref) = refs[:6]
     (field, stage, beside, edges) = refs[6:10]
     (held, inbox, sums, canvas, lat_taps, lon_taps, halves) = refs[10:17]
     strips, landed = refs[17:25], refs[25:33]
-    (windows, turned, total, flat, mixer, pieces, twin, parts, mine, gathered) = refs[33:43]
-    (load_sem, send_sem, recv_sem, field_send, field_recv) = refs[43:48]
-    halo_send, halo_recv, pair_send, pair_recv, part_send, part_recv, all_send, all_recv = refs[48:]
+    (windows, turned, total, flat, mixer, pieces, twin, parts, mine) = refs[33:42]
+    (load_sem, send_sem, recv_sem, field_send, field_recv) = refs[42:47]
+    halo_send, halo_recv, pair_send, pair_recv, part_send, part_recv, all_send, all_recv = refs[47:]
     devices = inbox.shape[0]
     row_total, channels = rows_ref.shape
     tile_lat, tile_lon = ig_ref.shape[:2]
@@ -83,6 +83,8 @@
     total[...] = jnp.zeros_like(total)
     rows, cols = tile_lat + 2, tile_lon + 2
     stage[...] = jnp.zeros_like(stage)
+    for margin in (slice(0, 8), slice(canvas.shape[1] - 8, canvas.shape[1])):
+        canvas[:, margin, :] = jnp.zeros((tall, 8, channels), f32)
     field[tall + 1] = jnp.zeros(field.shape[1:], bf16)
 
     @pl.when(lat == 0)
@@ -218,11 +220,13 @@
     for (copy, sends, _), (da, _) in zip(borders, ways):
         when(da, sends, copy.start)
 
+    def aligned(start, size):
+        if not isinstance(start, int):
+            start = pl.multiple_of(start, tile_lon)
+        return pl.ds(start, size)
+
     def turn(p):
-        at = p * tile_lon
-        if not isinstance(p, int):
-            at = pl.multiple_of(at, tile_lon)
-        turned[:, pl.ds(at, tile_lon)] = field[p].T
+        turned[:, aligned(p * tile_lon, tile_lon)] = field[p].T
 
     fast = math.gcd(tile_lat, 8)
 
@@ -253,7 +257,9 @@
         weight = jnp.exp(-(d * d) * inv)
         return jnp.where((tap >= 0.0) & (tap <= taps - 1.0), weight, 0.0)
 
-    def collect(q):
+    pad = reach
+
+    def collect(q, last):
         for i in range(group):
             peer = q * group + i
 
@@ -298,21 +304,27 @@
                     lhs.append(row.astype(bf16) * lon_taps[t : t + 16, :])
             out = jnp.dot(jnp.concatenate(lhs, axis=0), halves[...], preferred_element_type=f32)
             for j in range(stride):
-                sums[k * stride + j] += out[j * wide : (j + 1) * wide]
+                i = k * stride + j
+                row = sums[i] + out[j * wide : (j + 1) * wide]
+                if not last:
+                    sums[i] = row
+                    continue
+                left, right = row[:, 0:channels], row[:, channels : 2 * channels]
+                canvas[i, pad : pad + half, :] = left[0:half]
+                canvas[i, pad + half : pad + wide, :] = left[half:wide] + right[0 : wide - half]
+                canvas[i, pad + wide : pad + wide + half, :] = right[wide - half : wide]
             return 0
 
         lax.fori_loop(0, tall // stride, add, 0)
 
-    def border():
-        for (copy, _, takes), (da, _) in zip(borders, ways):
-            when(da, takes, copy.wait_recv)
-        for p in (*range(up), *range(up + tile_lat, tall + 2)):
-            turn(p)
-        slots = 2 * reach
-        some = 128 // slots
+    slots = 2 * reach
+    rows_at_once = 128 // slots
+    last_chunk = tall // rows_at_once - 1
+
+    def flank(chunks):
         for a in range(3):
-            for k in range(tall // some):
-                at = slice(a + k * some, a + (k + 1) * some)
+            for k in chunks:
+                at = slice(a + k * rows_at_once, a + (k + 1) * rows_at_once)
                 both = jnp.concatenate(
                     [field[at, 0:reach], field[at, tile_lon - reach : tile_lon]], axis=1
                 )
@@ -320,24 +332,18 @@
                     128, channels
                 ).T
 
+    def border():
+        for (copy, _, takes), (da, _) in zip(borders, ways):
+            when(da, takes, copy.wait_recv)
+        for p in (*range(up), *range(up + tile_lat, tall + 2)):
+            turn(p)
+        flank((0, last_chunk))
+
     for k, q in enumerate([order[3], order[2], order[0], order[1]] if groups == 4 else order[::-1]):
         if k == groups - 1:
-            border()
-        collect(q)
-
-    pad = reach
-
-    def join(i, _):
-        canvas[i, 0:pad, :] = jnp.zeros((pad, channels), f32)
-        canvas[i, pad : pad + half, :] = sums[i, 0:half, 0:channels]
-        canvas[i, pad + half : pad + wide, :] = (
-            sums[i, half:wide, 0:channels] + sums[i, 0 : wide - half, channels : 2 * channels]
-        )
-        canvas[i, pad + wide : pad + wide + half, :] = sums[i, wide - half : wide, channels : 2 * channels]
-        canvas[i, pad + wide + half : 2 * pad + wide + half, :] = jnp.zeros((pad, channels), f32)
-        return 0
-
-    lax.fori_loop(0, tall, join, 0)
+            flank(range(1, last_chunk))
+        collect(q, k == groups - 1)
+
     inset = before - 1
     edge = pad + inset
 
@@ -425,16 +431,20 @@
         start = k * depth
         lhs = jnp.concatenate(
             [
-                turned[:, pl.ds(pl.multiple_of(start + a * tile_lon, tile_lon), depth)]
+                turned[:, aligned(start + a * tile_lon, depth)]
                 for a in range(3)
             ],
             axis=0,
         )
-        rhs = windows[pl.ds(pl.multiple_of(start, tile_lon), depth), :]
+        rhs = windows[aligned(start, depth), :]
         total[...] += jnp.dot(lhs, rhs, preferred_element_type=f32)
         return 0
 
-    lax.fori_loop(0, tall // step, weigh, 0)
+    last_step = tall // step - 1
+    lax.fori_loop(1, last_step, weigh, 0)
+    border()
+    weigh(0, 0)
+    weigh(last_step, 0)
     for copy, _, _ in beside_halos:
         copy.wait_recv()
     lax.fori_loop(0, tall // some, shift_edges, 0)
@@ -574,13 +584,7 @@
     back = paired(kept, kept, 1)
     back.start()
 
-    def spill(d, _):
-        wg_ref[pl.ds(d * share, share), :] = gathered[d].astype(f32)
-        return 0
-
-    lax.fori_loop(core * chips, (core + 1) * chips, spill, 0)
     back.wait_recv()
-    lax.fori_loop(other * chips, (other + 1) * chips, spill, 0)
     for (copy, sends, _), (da, _) in zip(halos + borders, ways + ways[:2]):
         when(da, sends, copy.wait_send)
     swap.wait_send()
@@ -596,6 +600,18 @@
         lax.fori_loop(1, devices, body, 0)
 
     each(lambda peer: copy_to(peer, me).wait_send())
+
+
+def finish_kernel(grad_ref, shares_ref, grad_out, weight_out, flat, sem):
+    grad_copy = pltpu.make_async_copy(grad_ref, grad_out, sem.at[0])
+    grad_copy.start()
+    share = shares_ref.shape[1]
+    for d in range(shares_ref.shape[0]):
+        flat[d * share : (d + 1) * share, :] = shares_ref[d].astype(f32)
+    weight_copy = pltpu.make_async_copy(flat, weight_out, sem.at[1])
+    weight_copy.start()
+    grad_copy.wait()
+    weight_copy.wait()
 
 
 def shards(grad_rows, owner, lat_offset, lon_offset, position, live_count, features, conv_weight):
@@ -639,11 +655,11 @@
         features,
         conv_weight,
     )
-    input_grad, weight_grad = pl.pallas_call(
+    inner_grad, shares = pl.pallas_call(
         functools.partial(solve_kernel, capacity, lat_total, lon_total),
         out_shape=[
             jax.ShapeDtypeStruct((tile_lat, tile_lon, channels), bf16),
-            jax.ShapeDtypeStruct((flat_rows, channels), f32),
+            jax.ShapeDtypeStruct((device_total, share, channels), bf16),
         ],
         in_specs=[smem] + [pl.BlockSpec(memory_space=pltpu.HBM)] * 7,
         out_specs=[vmem] * 2,
@@ -673,7 +689,6 @@
             half_ring,
             half_ring,
             pltpu.VMEM((share, channels), bf16),
-            ring,
             dma((7,)),
             dma((device_total,)),
             dma((device_total,)),
@@ -693,6 +708,18 @@
         ),
         name="solve",
     )(live_count, *[pltpu.with_memory_space_constraint(x, pltpu.HBM) for x in operands])
+    input_grad, weight_grad = pl.pallas_call(
+        finish_kernel,
+        out_shape=[
+            jax.ShapeDtypeStruct((tile_lat, tile_lon, channels), bf16),
+            jax.ShapeDtypeStruct((flat_rows, channels), f32),
+        ],
+        in_specs=[vmem] * 2,
+        out_specs=[pl.BlockSpec(memory_space=pltpu.HBM)] * 2,
+        scratch_shapes=[pltpu.VMEM((flat_rows, channels), f32), dma((2,))],
+        compiler_params=pltpu.CompilerParams(vmem_limit_bytes=8 * 2**20),
+        name="finish",
+    )(inner_grad, shares)
     return input_grad, weight_grad.reshape(3, 3, channels, channels)
 
 

time: 54.1 us -> 51 us (0.943)
  local copies, waits for them, and re-layouts: 2.14 us -> 0 us
  Pallas kernels: 50.5 us -> 49.6 us
    pallas_call x1, Pallas kernels: 50.5 us -> 48.1 us  [shards(): pl.pallas_call(functools.partial(solve_kernel, capacity, lat_total, lon_t...]
    unnamed x2 -> x0, local copies, waits for them, and re-layouts: 2.14 us -> none
    pallas_call x0 -> x1, Pallas kernels: none -> 1.52 us  [shards(): pl.pallas_call(finish_kernel, out_shape=[jax.ShapeDtypeStruct((tile_lat,...]
where the time goes in v5:
time: 51 us; the launch traced here: 50.9 us
  Pallas kernels  49.6 us (97%)
  between operations  1.29 us (3%)
    pallas_call x1, Pallas kernels, shards(): pl.pallas_call(functools.partial(solve_kernel, capacity, lat_total, lon_t...  48.1 us
    pallas_call x1, Pallas kernels, shards(): pl.pallas_call(finish_kernel, out_shape=[jax.ShapeDtypeStruct((tile_lat,...  1.52 us

profile of v5, /device:TPU:1, one launch (start us, length us, event | category | flops | bytes accessed | tf_op | source)
XLA Modules:
  0.0 50.9 jit_solution(11449702173305000798)
XLA Ops:
  1.3 48.1 %solve.1 = (bf16[64,128,128]{2,1,0:T(8,128)(2,1)S(1)}, bf16[32,36,128]{2,1,0:T(8,128)(2,1)S(1)}) custom-call(s32[1]{0:T(128)S(6)} %copy.10.live_ref, bf16[1024,128]{1,0:T(8,128)(2,1)} %rows_hbm.1, s32[1,1024]{1,0:T(1,128)} %bitcast.5, s32[1,1024]{1,0:T(1,128)} %bitcast.6, s32[1,1024]{1,0:T(1,128)} %bitcast.7, bf16[2,1024]{1,0:T(2,128)(2,1)} %bitcast.8, ...), custom_call_target="tpu_custom_call" | custom-call | tf_op jit(solution)/shard_map/solve/pallas_call | solution.py:658
  49.3 1.5 %finish.1 = (bf16[64,128,128]{2,1,0:T(8,128)(2,1)}, f32[1152,128]{1,0:T(8,128)}) custom-call(bf16[64,128,128]{2,1,0:T(8,128)(2,1)S(1)} %get-tuple-element.6.grad_ref, bf16[32,36,128]{2,1,0:T(8,128)(2,1)S(1)} %get-tuple-element.7.shares_ref), custom_call_target="tpu_custom_call" | custom-call | tf_op jit(solution)/shard_map/finish/pallas_call | solution.py:711

commit v6 on v5

--- a/solution.py
+++ b/solution.py
@@ -60,11 +60,19 @@
 
     barrier = pltpu.get_barrier_semaphore()
 
-    def greet(k, _):
-        pl.semaphore_signal(
-            barrier, inc=1, device_id=place((me + k) % devices), device_id_type=pl.DeviceIdType.MESH
-        )
-        return 0
+    if groups == 4:
+        order = [3 - ours, (ours + 2) % 4, ours + 1 - 2 * (ours % 2), ours]
+    else:
+        order = [(ours + groups // 2 + k) % groups for k in range(groups)]
+    for q in order:
+        for i in range(group):
+            peer = q * group + i
+
+            @pl.when(peer != me)
+            def _():
+                pl.semaphore_signal(
+                    barrier, inc=1, device_id=place(peer), device_id_type=pl.DeviceIdType.MESH
+                )
 
     loads = [
         pltpu.make_async_copy(src, dst, load_sem.at[k])
@@ -77,7 +85,6 @@
     ]
     for load in loads:
         load.start()
-    lax.fori_loop(1, devices, greet, 0)
     sums[...] = jnp.zeros_like(sums)
     mixer[...] = jnp.zeros_like(mixer)
     total[...] = jnp.zeros_like(total)
@@ -171,13 +178,8 @@
             def _():
                 copy_to(peer, me).start()
 
-    if groups == 4:
-        order = [3 - ours, (ours + 2) % 4, ours + 1 - 2 * (ours % 2), ours]
-    else:
-        order = [(ours + groups // 2 + k) % groups for k in range(groups)]
     per = group // chunk
-    steps = [(q, c) for q in order for c in range(per)]
-    first_of = [q * group + c * chunk for q, c in steps]
+    first_of = [q * group + ((c + lon) % per) * chunk for q in order for c in range(per)]
     early = len(first_of) // 2
     for first in first_of[:early]:
         build(first)
@@ -259,17 +261,17 @@
 
     pad = reach
 
-    def collect(q, last):
-        for i in range(group):
-            peer = q * group + i
+    def collect(first, count, last):
+        size = count * capacity
+        for i in range(count):
+            peer = first + i
 
             @pl.when(peer != me)
             def _():
                 copy_to(peer, peer).wait_recv()
 
-        first = q * group
         infos = []
-        for v in range(span // 128):
+        for v in range(size // 128):
             at = first + v * fold
             info = inbox[at, capacity : capacity + geom_rows, :].astype(f32)
             for t in range(1, fold):
@@ -280,9 +282,9 @@
         info = jnp.concatenate(infos, axis=1)
         lat_frac, lon_frac, row_at, col_at = (info[k : k + 1] for k in range(4))
         right = jnp.where(col_at >= half, 1.0, 0.0)
-        lat_taps[...] = taps_of(line_lat, row_at, lat_frac).astype(bf16).astype(f32)
-        lon_taps[...] = taps_of(line_lon, col_at - right * half, lon_frac).astype(bf16)
-        for v in range(span // 128):
+        lat_taps[:, 0:size] = taps_of(line_lat[:, 0:size], row_at, lat_frac).astype(bf16).astype(f32)
+        lon_taps[:, 0:size] = taps_of(line_lon[:, 0:size], col_at - right * half, lon_frac).astype(bf16)
+        for v in range(size // 128):
             side = jnp.broadcast_to(right[:, v * 128 : (v + 1) * 128], (128, 128)).T.astype(bf16)
             rows = jnp.concatenate(
                 [inbox[first + v * fold + t, 0:capacity, :] for t in range(fold)], axis=0
@@ -296,13 +298,13 @@
             lhs = []
             for j in range(0, stride, 2):
                 pair = [
-                    jnp.broadcast_to(lat_taps[pl.ds(k * stride + j + n, 1), :], (8, span))
+                    jnp.broadcast_to(lat_taps[pl.ds(k * stride + j + n, 1), 0:size], (8, size))
                     for n in range(2)
                 ]
                 for t in range(0, 2 * wide, 16):
                     row = jnp.concatenate([pair[t // wide], pair[(t + 8) // wide]], axis=0)
-                    lhs.append(row.astype(bf16) * lon_taps[t : t + 16, :])
-            out = jnp.dot(jnp.concatenate(lhs, axis=0), halves[...], preferred_element_type=f32)
+                    lhs.append(row.astype(bf16) * lon_taps[t : t + 16, 0:size])
+            out = jnp.dot(jnp.concatenate(lhs, axis=0), halves[0:size, :], preferred_element_type=f32)
             for j in range(stride):
                 i = k * stride + j
                 row = sums[i] + out[j * wide : (j + 1) * wide]
@@ -339,10 +341,12 @@
             turn(p)
         flank((0, last_chunk))
 
-    for k, q in enumerate([order[3], order[2], order[0], order[1]] if groups == 4 else order[::-1]):
-        if k == groups - 1:
-            flank(range(1, last_chunk))
-        collect(q, k == groups - 1)
+    arrival = [order[3], order[2], order[0], order[1]] if groups == 4 else order[::-1]
+    for q in arrival[:-1]:
+        collect(q * group, group, False)
+    flank(range(1, last_chunk))
+    for c in range(per):
+        collect(arrival[-1] * group + ((c + lon) % per) * chunk, chunk, c == per - 1)
 
     inset = before - 1
     edge = pad + inset
@@ -393,12 +397,21 @@
         if da != 0:
             pl.when(sends)(copy.start)
     chips = devices // 2
-    at = lat * lon_total + lon
-    core, chip = at % 2, at // 2
+    planes = lon_total // 2
+    outer = planes // 4
+    inner = planes - 2 * outer
+    roots = lat_total * inner
+    plane, core = lon // 2, lon % 2
+    chip = lat * planes + plane
     other = 1 - core
+    is_root = (plane >= outer) & (plane < planes - outer)
+    root = lat * inner + plane - outer
 
     def seat(peer):
-        return (peer // lon_total, peer % lon_total)
+        return (peer // planes, (peer % planes) * 2 + core)
+
+    def chip_of(r):
+        return (r // inner) * planes + r % inner + outer
 
     def shift(i, _):
         at = pl.ds(pl.multiple_of(i * tile_lon, tile_lon), tile_lon)
@@ -461,7 +474,7 @@
         pieces[d] = flat[pl.ds(d * share, share), :].astype(bf16)
         return 0
 
-    lax.fori_loop(0, devices, cut, 0)
+    lax.fori_loop(0, 2 * roots, cut, 0)
     part = math.gcd(tile_lat // 2, 8)
     strides = tile_lat // 2 // part
     first = strides // 2
@@ -523,29 +536,41 @@
             dst_ref=dst,
             send_sem=pair_send.at[n],
             recv_sem=pair_recv.at[n],
-            device_id=seat(chip * 2 + other),
+            device_id=(lat, plane * 2 + other),
             device_id_type=pl.DeviceIdType.MESH,
         )
 
-    def scattered(peer, slot):
+    def scattered(r, slot):
         return pltpu.make_async_remote_copy(
-            src_ref=pieces.at[core * chips + peer],
+            src_ref=pieces.at[core * roots + r],
             dst_ref=parts.at[slot],
-            send_sem=part_send.at[peer],
+            send_sem=part_send.at[r],
             recv_sem=part_recv.at[slot],
-            device_id=seat(peer * 2 + core),
+            device_id=seat(chip_of(r)),
             device_id_type=pl.DeviceIdType.MESH,
         )
 
-    def shared(peer, slot):
+    def shared(peer, r):
         return pltpu.make_async_remote_copy(
             src_ref=mine,
-            dst_ref=gathered.at[core * chips + slot],
+            dst_ref=gathered.at[core * roots + r],
             send_sem=all_send.at[peer],
-            recv_sem=all_recv.at[slot],
-            device_id=seat(peer * 2 + core),
+            recv_sem=all_recv.at[r],
+            device_id=seat(peer),
             device_id_type=pl.DeviceIdType.MESH,
         )
+
+    def each_root(fn):
+        def body(k, _):
+            r = (chip + k) % roots
+
+            @pl.when(chip_of(r) != chip)
+            def _():
+                fn(r)
+
+            return 0
+
+        lax.fori_loop(0, roots, body, 0)
 
     def each_chip(fn):
         def body(k, _):
@@ -554,43 +579,50 @@
 
         lax.fori_loop(1, chips, body, 0)
 
-    swap = paired(pieces.at[pl.ds(other * chips, chips)], twin, 0)
+    swap = paired(pieces.at[pl.ds(other * roots, roots)], twin, 0)
     swap.start()
     swap.wait_recv()
 
     def merge(p, _):
-        at = core * chips + p
+        at = core * roots + p
         pieces[at] = (flat[pl.ds(at * share, share), :] + twin[p].astype(f32)).astype(bf16)
         return 0
 
-    lax.fori_loop(0, chips, merge, 0)
-    each_chip(lambda peer: scattered(peer, chip).start())
+    lax.fori_loop(0, roots, merge, 0)
+    each_root(lambda r: scattered(r, chip).start())
     settle()
     lax.fori_loop(0, first, apply, 0)
-    parts[chip] = pieces[core * chips + chip]
-    each_chip(lambda peer: scattered(peer, peer).wait_recv())
-
-    def gather_sum(p, acc):
-        return acc + parts[p].astype(f32)
-
-    mine[...] = lax.fori_loop(
-        0, chips, gather_sum, jnp.zeros((share, channels), f32)
-    ).astype(bf16)
-    each_chip(lambda peer: shared(peer, chip).start())
-    gathered[core * chips + chip] = mine[...]
+
+    @pl.when(is_root)
+    def _():
+        parts[chip] = pieces[core * roots + root]
+        each_chip(lambda peer: scattered(root, peer).wait_recv())
+
+        def gather_sum(p, acc):
+            return acc + parts[p].astype(f32)
+
+        mine[...] = lax.fori_loop(
+            0, chips, gather_sum, jnp.zeros((share, channels), f32)
+        ).astype(bf16)
+        each_chip(lambda peer: shared(peer, root).start())
+        gathered[core * roots + root] = mine[...]
+
     lax.fori_loop(first, strides, apply, 0)
-    each_chip(lambda peer: shared(peer, peer).wait_recv())
-    kept = gathered.at[pl.ds(core * chips, chips)]
+    each_root(lambda r: shared(chip, r).wait_recv())
+    kept = gathered.at[pl.ds(core * roots, roots)]
     back = paired(kept, kept, 1)
     back.start()
-
     back.wait_recv()
     for (copy, sends, _), (da, _) in zip(halos + borders, ways + ways[:2]):
         when(da, sends, copy.wait_send)
     swap.wait_send()
     back.wait_send()
-    each_chip(lambda peer: scattered(peer, chip).wait_send())
-    each_chip(lambda peer: shared(peer, chip).wait_send())
+    each_root(lambda r: scattered(r, chip).wait_send())
+
+    @pl.when(is_root)
+    def _():
+        each_chip(lambda peer: shared(peer, root).wait_send())
+
 
     def each(fn):
         def body(k, _):
@@ -641,9 +673,9 @@
     ]
     message = (device_total, capacity + geom_rows, channels)
     flat_rows = 9 * channels
-    share = flat_rows // device_total
-    ring = pltpu.VMEM((device_total, share, channels), bf16)
-    half_ring = pltpu.VMEM((device_total // 2, share, channels), bf16)
+    chips = device_total // 2
+    roots = lat_total * (lon_total // 2 - 2 * (lon_total // 8))
+    share = flat_rows // (2 * roots)
     dma = pltpu.SemaphoreType.DMA
     places = [pltpu.VMEM(shape + (channels,), bf16) for shape in strip_shapes]
     operands = (
@@ -659,7 +691,7 @@
         functools.partial(solve_kernel, capacity, lat_total, lon_total),
         out_shape=[
             jax.ShapeDtypeStruct((tile_lat, tile_lon, channels), bf16),
-            jax.ShapeDtypeStruct((device_total, share, channels), bf16),
+            jax.ShapeDtypeStruct((2 * roots, share, channels), bf16),
         ],
         in_specs=[smem] + [pl.BlockSpec(memory_space=pltpu.HBM)] * 7,
         out_specs=[vmem] * 2,
@@ -685,9 +717,9 @@
             pltpu.VMEM((3 * channels, 3 * channels), f32),
             pltpu.VMEM((flat_rows, channels), f32),
             pltpu.VMEM((4 * 3 * channels, 2 * channels), bf16),
-            ring,
-            half_ring,
-            half_ring,
+            pltpu.VMEM((2 * roots, share, channels), bf16),
+            pltpu.VMEM((roots, share, channels), bf16),
+            pltpu.VMEM((chips, share, channels), bf16),
             pltpu.VMEM((share, channels), bf16),
             dma((7,)),
             dma((device_total,)),
@@ -698,10 +730,10 @@
             dma((8,)),
             dma((2,)),
             dma((2,)),
-            dma((device_total // 2,)),
-            dma((device_total // 2,)),
-            dma((device_total // 2,)),
-            dma((device_total // 2,)),
+            dma((roots,)),
+            dma((chips,)),
+            dma((chips,)),
+            dma((roots,)),
         ],
         compiler_params=pltpu.CompilerParams(
             vmem_limit_bytes=44 * 2**20, collective_id=0, has_side_effects=True

time: 51 us -> 51.3 us (level)
  no operation moved by 1% of the time
where the time goes in v6:
time: 51.3 us; the launch traced here: 51.2 us
  Pallas kernels  49.9 us (97%)
  between operations  1.29 us (3%)
    pallas_call x1, Pallas kernels, shards(): pl.pallas_call(functools.partial(solve_kernel, capacity, lat_total, lon_t...  48.4 us
    pallas_call x1, Pallas kernels, shards(): pl.pallas_call(finish_kernel, out_shape=[jax.ShapeDtypeStruct((tile_lat,...  1.52 us

profile of v6, /device:TPU:1, one launch (start us, length us, event | category | flops | bytes accessed | tf_op | source)
XLA Modules:
  0.0 51.2 jit_solution(10799444103466134542)
XLA Ops:
  1.3 48.4 %solve.1 = (bf16[64,128,128]{2,1,0:T(8,128)(2,1)S(1)}, bf16[16,72,128]{2,1,0:T(8,128)(2,1)S(1)}) custom-call(s32[1]{0:T(128)S(6)} %copy.10.live_ref, bf16[1024,128]{1,0:T(8,128)(2,1)} %rows_hbm.1, s32[1,1024]{1,0:T(1,128)} %bitcast.5, s32[1,1024]{1,0:T(1,128)} %bitcast.6, s32[1,1024]{1,0:T(1,128)} %bitcast.7, bf16[2,1024]{1,0:T(2,128)(2,1)} %bitcast.8, ...), custom_call_target="tpu_custom_call" | custom-call | tf_op jit(solution)/shard_map/solve/pallas_call | solution.py:690
  49.6 1.5 %finish.1 = (bf16[64,128,128]{2,1,0:T(8,128)(2,1)}, f32[1152,128]{1,0:T(8,128)}) custom-call(bf16[64,128,128]{2,1,0:T(8,128)(2,1)S(1)} %get-tuple-element.6.grad_ref, bf16[16,72,128]{2,1,0:T(8,128)(2,1)S(1)} %get-tuple-element.7.shares_ref), custom_call_target="tpu_custom_call" | custom-call | tf_op jit(solution)/shard_map/finish/pallas_call | solution.py:743

commit v7 on v6

--- a/solution.py
+++ b/solution.py
@@ -60,19 +60,11 @@
 
     barrier = pltpu.get_barrier_semaphore()
 
-    if groups == 4:
-        order = [3 - ours, (ours + 2) % 4, ours + 1 - 2 * (ours % 2), ours]
-    else:
-        order = [(ours + groups // 2 + k) % groups for k in range(groups)]
-    for q in order:
-        for i in range(group):
-            peer = q * group + i
-
-            @pl.when(peer != me)
-            def _():
-                pl.semaphore_signal(
-                    barrier, inc=1, device_id=place(peer), device_id_type=pl.DeviceIdType.MESH
-                )
+    def greet(k, _):
+        pl.semaphore_signal(
+            barrier, inc=1, device_id=place((me + k) % devices), device_id_type=pl.DeviceIdType.MESH
+        )
+        return 0
 
     loads = [
         pltpu.make_async_copy(src, dst, load_sem.at[k])
@@ -85,6 +77,7 @@
     ]
     for load in loads:
         load.start()
+    lax.fori_loop(1, devices, greet, 0)
     sums[...] = jnp.zeros_like(sums)
     mixer[...] = jnp.zeros_like(mixer)
     total[...] = jnp.zeros_like(total)
@@ -178,8 +171,13 @@
             def _():
                 copy_to(peer, me).start()
 
+    if groups == 4:
+        order = [(ours + 2) % 4, 3 - ours, ours + 1 - 2 * (ours % 2), ours]
+    else:
+        order = [(ours + groups // 2 + k) % groups for k in range(groups)]
     per = group // chunk
-    first_of = [q * group + ((c + lon) % per) * chunk for q in order for c in range(per)]
+    steps = [(q, c) for q in order for c in range(per)]
+    first_of = [q * group + c * chunk for q, c in steps]
     early = len(first_of) // 2
     for first in first_of[:early]:
         build(first)
@@ -251,7 +249,7 @@
     lanes = lax.broadcasted_iota(jnp.int32, (8, 128), 1) // capacity
     wide = sums.shape[1]
     line_lon = jnp.where(line_lon >= wide, line_lon - wide, line_lon)
-    stride = next(n for n in (24, 12, 8, 4, 2) if tall % n == 0)
+    stride = next(n for n in (36, 24, 12, 8, 4, 2) if tall % n == 0)
 
     def taps_of(line, base, frac):
         tap = line - base
@@ -261,17 +259,17 @@
 
     pad = reach
 
-    def collect(first, count, last):
-        size = count * capacity
-        for i in range(count):
-            peer = first + i
+    def collect(q, last):
+        for i in range(group):
+            peer = q * group + i
 
             @pl.when(peer != me)
             def _():
                 copy_to(peer, peer).wait_recv()
 
+        first = q * group
         infos = []
-        for v in range(size // 128):
+        for v in range(span // 128):
             at = first + v * fold
             info = inbox[at, capacity : capacity + geom_rows, :].astype(f32)
             for t in range(1, fold):
@@ -282,9 +280,9 @@
         info = jnp.concatenate(infos, axis=1)
         lat_frac, lon_frac, row_at, col_at = (info[k : k + 1] for k in range(4))
         right = jnp.where(col_at >= half, 1.0, 0.0)
-        lat_taps[:, 0:size] = taps_of(line_lat[:, 0:size], row_at, lat_frac).astype(bf16).astype(f32)
-        lon_taps[:, 0:size] = taps_of(line_lon[:, 0:size], col_at - right * half, lon_frac).astype(bf16)
-        for v in range(size // 128):
+        lat_taps[...] = taps_of(line_lat, row_at, lat_frac).astype(bf16).astype(f32)
+        lon_taps[...] = taps_of(line_lon, col_at - right * half, lon_frac).astype(bf16)
+        for v in range(span // 128):
             side = jnp.broadcast_to(right[:, v * 128 : (v + 1) * 128], (128, 128)).T.astype(bf16)
             rows = jnp.concatenate(
                 [inbox[first + v * fold + t, 0:capacity, :] for t in range(fold)], axis=0
@@ -298,13 +296,13 @@
             lhs = []
             for j in range(0, stride, 2):
                 pair = [
-                    jnp.broadcast_to(lat_taps[pl.ds(k * stride + j + n, 1), 0:size], (8, size))
+                    jnp.broadcast_to(lat_taps[pl.ds(k * stride + j + n, 1), :], (8, span))
                     for n in range(2)
                 ]
                 for t in range(0, 2 * wide, 16):
                     row = jnp.concatenate([pair[t // wide], pair[(t + 8) // wide]], axis=0)
-                    lhs.append(row.astype(bf16) * lon_taps[t : t + 16, 0:size])
-            out = jnp.dot(jnp.concatenate(lhs, axis=0), halves[0:size, :], preferred_element_type=f32)
+                    lhs.append(row.astype(bf16) * lon_taps[t : t + 16, :])
+            out = jnp.dot(jnp.concatenate(lhs, axis=0), halves[...], preferred_element_type=f32)
             for j in range(stride):
                 i = k * stride + j
                 row = sums[i] + out[j * wide : (j + 1) * wide]
@@ -341,12 +339,10 @@
             turn(p)
         flank((0, last_chunk))
 
-    arrival = [order[3], order[2], order[0], order[1]] if groups == 4 else order[::-1]
-    for q in arrival[:-1]:
-        collect(q * group, group, False)
-    flank(range(1, last_chunk))
-    for c in range(per):
-        collect(arrival[-1] * group + ((c + lon) % per) * chunk, chunk, c == per - 1)
+    for k, q in enumerate([order[3], order[2], order[0], order[1]] if groups == 4 else order[::-1]):
+        if k == groups - 1:
+            flank(range(1, last_chunk))
+        collect(q, k == groups - 1)
 
     inset = before - 1
     edge = pad + inset
@@ -477,7 +473,7 @@
     lax.fori_loop(0, 2 * roots, cut, 0)
     part = math.gcd(tile_lat // 2, 8)
     strides = tile_lat // 2 // part
-    first = strides // 2
+    first = strides // 4
 
     def apply(k, _):
         lhs = jnp.concatenate(

time: 51.3 us -> 49.4 us (0.963)
  Pallas kernels: 49.9 us -> 48 us
    pallas_call x1, Pallas kernels: 48.4 us -> 46.5 us  [shards(): pl.pallas_call(functools.partial(solve_kernel, capacity, lat_total, lon_t...]
where the time goes in v7:
time: 49.4 us; the launch traced here: 49.3 us
  Pallas kernels  48 us (97%)
  between operations  1.29 us (3%)
    pallas_call x1, Pallas kernels, shards(): pl.pallas_call(functools.partial(solve_kernel, capacity, lat_total, lon_t...  46.5 us
    pallas_call x1, Pallas kernels, shards(): pl.pallas_call(finish_kernel, out_shape=[jax.ShapeDtypeStruct((tile_lat,...  1.52 us

profile of v7, /device:TPU:1, one launch (start us, length us, event | category | flops | bytes accessed | tf_op | source)
XLA Modules:
  0.0 49.3 jit_solution(4254615350962550544)
XLA Ops:
  1.3 46.5 %solve.1 = (bf16[64,128,128]{2,1,0:T(8,128)(2,1)S(1)}, bf16[16,72,128]{2,1,0:T(8,128)(2,1)S(1)}) custom-call(s32[1]{0:T(128)S(6)} %copy.10.live_ref, bf16[1024,128]{1,0:T(8,128)(2,1)} %rows_hbm.1, s32[1,1024]{1,0:T(1,128)} %bitcast.5, s32[1,1024]{1,0:T(1,128)} %bitcast.6, s32[1,1024]{1,0:T(1,128)} %bitcast.7, bf16[2,1024]{1,0:T(2,128)(2,1)} %bitcast.8, ...), custom_call_target="tpu_custom_call" | custom-call | tf_op jit(solution)/shard_map/solve/pallas_call | solution.py:686
  47.7 1.5 %finish.1 = (bf16[64,128,128]{2,1,0:T(8,128)(2,1)}, f32[1152,128]{1,0:T(8,128)}) custom-call(bf16[64,128,128]{2,1,0:T(8,128)(2,1)S(1)} %get-tuple-element.6.grad_ref, bf16[16,72,128]{2,1,0:T(8,128)(2,1)S(1)} %get-tuple-element.7.shares_ref), custom_call_target="tpu_custom_call" | custom-call | tf_op jit(solution)/shard_map/finish/pallas_call | solution.py:739

commit v8 on v7

--- a/solution.py
+++ b/solution.py
@@ -409,15 +409,19 @@
     def chip_of(r):
         return (r // inner) * planes + r % inner + outer
 
-    def shift(i, _):
+    def shift_row(i):
         at = pl.ds(pl.multiple_of(i * tile_lon, tile_lon), tile_lon)
         for b in range(3):
             windows[at, b * channels : (b + 1) * channels] = canvas[
                 i, edge + 2 - b : edge + 2 - b + tile_lon, :
             ].astype(bf16)
-        return 0
-
-    lax.fori_loop(0, tall, shift, 0)
+
+    def shift(k, _):
+        for j in range(2):
+            shift_row(2 * k + j)
+        return 0
+
+    lax.fori_loop(0, tall // 2, shift, 0)
 
     def shift_edges(k, _):
         for j in range(some):
@@ -470,10 +474,9 @@
         pieces[d] = flat[pl.ds(d * share, share), :].astype(bf16)
         return 0
 
-    lax.fori_loop(0, 2 * roots, cut, 0)
+    lax.fori_loop(0, 2 * roots, cut, 0, unroll=4)
     part = math.gcd(tile_lat // 2, 8)
     strides = tile_lat // 2 // part
-    first = strides // 4
 
     def apply(k, _):
         lhs = jnp.concatenate(
@@ -524,7 +527,7 @@
 
             when(da, takes, take)
 
-        lax.fori_loop(inset, inset + rows, shift, 0)
+        lax.fori_loop(inset // 2, (inset + rows) // 2, shift, 0)
 
     def paired(src, dst, n):
         return pltpu.make_async_remote_copy(
@@ -584,10 +587,8 @@
         pieces[at] = (flat[pl.ds(at * share, share), :] + twin[p].astype(f32)).astype(bf16)
         return 0
 
-    lax.fori_loop(0, roots, merge, 0)
+    lax.fori_loop(0, roots, merge, 0, unroll=4)
     each_root(lambda r: scattered(r, chip).start())
-    settle()
-    lax.fori_loop(0, first, apply, 0)
 
     @pl.when(is_root)
     def _():
@@ -598,12 +599,13 @@
             return acc + parts[p].astype(f32)
 
         mine[...] = lax.fori_loop(
-            0, chips, gather_sum, jnp.zeros((share, channels), f32)
+            0, chips, gather_sum, jnp.zeros((share, channels), f32), unroll=4
         ).astype(bf16)
         each_chip(lambda peer: shared(peer, root).start())
         gathered[core * roots + root] = mine[...]
 
-    lax.fori_loop(first, strides, apply, 0)
+    settle()
+    lax.fori_loop(0, strides, apply, 0)
     each_root(lambda r: shared(chip, r).wait_recv())
     kept = gathered.at[pl.ds(core * roots, roots)]
     back = paired(kept, kept, 1)

time: 49.4 us -> 49.3 us (level)
  no operation moved by 1% of the time
where the time goes in v8:
time: 49.3 us; the launch traced here: 49 us
  Pallas kernels  47.8 us (97%)
  between operations  1.29 us (3%)
    pallas_call x1, Pallas kernels, shards(): pl.pallas_call(functools.partial(solve_kernel, capacity, lat_total, lon_t...  46.2 us
    pallas_call x1, Pallas kernels, shards(): pl.pallas_call(finish_kernel, out_shape=[jax.ShapeDtypeStruct((tile_lat,...  1.52 us

profile of v8, /device:TPU:1, one launch (start us, length us, event | category | flops | bytes accessed | tf_op | source)
XLA Modules:
  0.0 49.0 jit_solution(14872056900139613939)
XLA Ops:
  1.3 46.2 %solve.1 = (bf16[64,128,128]{2,1,0:T(8,128)(2,1)S(1)}, bf16[16,72,128]{2,1,0:T(8,128)(2,1)S(1)}) custom-call(s32[1]{0:T(128)S(6)} %copy.10.live_ref, bf16[1024,128]{1,0:T(8,128)(2,1)} %rows_hbm.1, s32[1,1024]{1,0:T(1,128)} %bitcast.5, s32[1,1024]{1,0:T(1,128)} %bitcast.6, s32[1,1024]{1,0:T(1,128)} %bitcast.7, bf16[2,1024]{1,0:T(2,128)(2,1)} %bitcast.8, ...), custom_call_target="tpu_custom_call" | custom-call | tf_op jit(solution)/shard_map/solve/pallas_call | solution.py:688
  47.5 1.5 %finish.1 = (bf16[64,128,128]{2,1,0:T(8,128)(2,1)}, f32[1152,128]{1,0:T(8,128)}) custom-call(bf16[64,128,128]{2,1,0:T(8,128)(2,1)S(1)} %get-tuple-element.6.grad_ref, bf16[16,72,128]{2,1,0:T(8,128)(2,1)S(1)} %get-tuple-element.7.shares_ref), custom_call_target="tpu_custom_call" | custom-call | tf_op jit(solution)/shard_map/finish/pallas_call | solution.py:741
